TPU v7x, 256 devices: a whole 4x4x8 slice. The times are simulated.
256 devices in a mesh: dp: 8 (over z_lo, x), seq: 32 (over y, z_hi, core).
Axes of the slice: x: 4, y: 4, z: 8 (z_hi: 4, z_lo: 2; z = z_hi * 2 + z_lo), core: 2. Of those that a mesh axis runs over, the one named last changes fastest.
Arguments:
- queries: bfloat16 [8, 4096, 4096], P('dp', 'seq'), may hold values from -5 to 5
- rotated_key_rows: bfloat16 [8, 4096, 512], P('dp', 'seq'), may hold values from -5 to 5
- hidden_states: bfloat16 [8, 4096, 8192], P('dp', 'seq'), may hold values from -6 to 6
- block_order: int32 [64], replicated, may hold values from 0 to 63, each once
- first_weight: bfloat16 [8192, 512], replicated, may hold values from -0.0625 to 0.0625
- first_bias: float32 [512], replicated, may hold values from -3 to 3
- output_weight: bfloat16 [4, 512], replicated, may hold values from -0.25 to 0.25
- output_bias: float32 [4], replicated, may hold values from -1 to 1
Outputs:
- token_attention_mass: float32 [8, 4, 4096], P('dp', None, 'seq')
- loss_value: float32 [], replicated
- step_first: float32 [8192, 512], P('seq')
- output_weight_step: float32 [4, 512], replicated
- step_bias: float32 [512], replicated
- grad_bias: float32 [4], replicated
All inputs are finite; a program needn't handle non-finite values.
Results may differ from a plain program's by a relative error of at most 0.0023.
Values may be sent and summed in bfloat16 or wider, within the bound.
A program may use at most 64 MiB of HBM per device.

v0:
```python
import math

import jax
import jax.numpy as jnp
from jax import lax
from jax.sharding import PartitionSpec as P

D = 8192
KEY_VALUE_HEADS = 4
HEAD_SIZE = 128
RETAIN_HIDDEN = 512
BLK = 64
QUERY_GROUP_SIZE = 8


def key_places(block_order, offset, amount):
    row_ids = offset + lax.iota(jnp.int32, amount)
    block_ids = row_ids // BLK
    block_table = lax.iota(jnp.int32, block_order.shape[0])
    anchor = jnp.sum(
        jnp.where(block_ids[:, None] == block_table[None, :], block_order[None, :], 0), axis=1
    )
    return anchor * BLK + row_ids % BLK


def raw_scores(head_queries, mass_portion):
    head_keys = mass_portion.reshape(mass_portion.shape[0], KEY_VALUE_HEADS, HEAD_SIZE)
    return jnp.einsum(
        "tkgd,nkd->kgtn", head_queries, head_keys, preferred_element_type=jnp.float32
    ) * HEAD_SIZE ** (-0.5)


def blockwise(mass_portion, offset, update, carried):
    rows_here = mass_portion.shape[0]
    inner = math.gcd(rows_here, BLK)

    def visit_block(step_index, running):
        local_start = step_index * inner
        sub_rows = lax.dynamic_slice_in_dim(mass_portion, local_start, inner, 0)
        return update(running, sub_rows, offset + local_start)

    return lax.fori_loop(0, rows_here // inner, visit_block, carried)


def normalizer_step(running, mass_portion, key_start, head_queries, query_pos, block_order):
    highest, summed = running
    key_pos = key_places(block_order, key_start, mass_portion.shape[0])

    def normalizer_compute_step():
        scores = raw_scores(head_queries, mass_portion)
        visible = query_pos[:, None] >= key_pos[None, :]
        masked = jnp.where(visible, scores, -1e30)
        raised = jnp.maximum(highest, jnp.max(masked, axis=-1))
        exponents = jnp.where(visible, jnp.exp(masked - raised[..., None]), 0.0)
        return (raised, summed * jnp.exp(highest - raised) + jnp.sum(exponents, axis=-1))

    return lax.cond(
        jnp.min(key_pos) > jnp.max(query_pos), lambda: (highest, summed), normalizer_compute_step
    )


def mass_step(mass_portion, key_start, head_queries, query_pos, log_total, block_order):
    amount = mass_portion.shape[0]
    key_pos = key_places(block_order, key_start, amount)

    def mass_compute_step():
        scores = raw_scores(head_queries, mass_portion)
        visible = query_pos[:, None] >= key_pos[None, :]
        masked = jnp.where(visible, scores, -1e30)
        weights = jnp.where(visible, jnp.exp(masked - log_total[..., None]), 0.0)
        return jnp.sum(weights, axis=(1, 2)) / QUERY_GROUP_SIZE

    return lax.cond(
        jnp.min(key_pos) > jnp.max(query_pos),
        lambda: jnp.zeros((KEY_VALUE_HEADS, amount), jnp.float32),
        mass_compute_step,
    )


def normalized_scores(value_rows, square_sum, entries):
    return value_rows / jnp.sqrt(square_sum / entries + 1e-06)


def per_device(
    queries,
    rotated_key_rows,
    hidden_states,
    block_order,
    first_weight,
    first_bias,
    output_weight,
    output_bias,
):
    local_row_slice = queries.shape[1]
    total_length = local_row_slice * lax.axis_size("seq")
    head_queries = queries.reshape(local_row_slice, KEY_VALUE_HEADS, QUERY_GROUP_SIZE, HEAD_SIZE)
    local_key_rows = rotated_key_rows.reshape(local_row_slice, KEY_VALUE_HEADS * HEAD_SIZE)
    query_pos = key_places(block_order, lax.axis_index("seq") * local_row_slice, local_row_slice)
    start_state = (
        jnp.full((KEY_VALUE_HEADS, QUERY_GROUP_SIZE, local_row_slice), -1e30, jnp.float32),
        jnp.zeros((KEY_VALUE_HEADS, QUERY_GROUP_SIZE, local_row_slice), jnp.float32),
    )

    def norm_update(running, sub_rows, key_start):
        return normalizer_step(running, sub_rows, key_start, head_queries, query_pos, block_order)

    empty_mass = jnp.zeros((KEY_VALUE_HEADS, total_length), jnp.float32)
    keys_whole = lax.all_gather(local_key_rows, "seq", axis=0, tiled=True)
    highest, summed = blockwise(keys_whole, 0, norm_update, start_state)
    log_total = highest + jnp.log(summed)

    def add_kept(collected, sub_rows, key_start):
        term = mass_step(sub_rows, key_start, head_queries, query_pos, log_total, block_order)
        return lax.dynamic_update_slice_in_dim(collected, term, key_start, 1)

    column_mass = blockwise(keys_whole, 0, add_kept, empty_mass)
    key_attention_mass = lax.psum_scatter(column_mass, "seq", scatter_dimension=1, tiled=True)
    tokens_in = hidden_states.reshape(local_row_slice, hidden_states.shape[2])
    pre_act = jnp.dot(tokens_in, first_weight, preferred_element_type=jnp.float32) + first_bias
    hidden = jax.nn.silu(pre_act).astype(jnp.bfloat16)
    predicted_scores = (
        lax.dot_general(
            output_weight, hidden, (((1,), (1,)), ((), ())), preferred_element_type=jnp.float32
        )
        + output_bias[:, None]
    )
    score_residue = predicted_scores - jnp.log(1.0 + key_attention_mass)
    loss_part = 0.5 * jnp.sum(score_residue * score_residue) / total_length
    out_grad = score_residue / total_length
    bias_part = jnp.sum(out_grad, axis=1)
    second_part = jnp.dot(out_grad, hidden.astype(jnp.float32), precision=lax.Precision.HIGHEST)
    back_grad = jnp.dot(
        out_grad.T, output_weight.astype(jnp.float32), precision=lax.Precision.HIGHEST
    )
    gate_value = jax.nn.sigmoid(pre_act)
    slope_grad = back_grad * gate_value * (1.0 + pre_act * (1.0 - gate_value))
    first_bias_part = jnp.sum(slope_grad, axis=0)
    slope_half = slope_grad.astype(jnp.bfloat16)
    columns_all = lax.all_to_all(tokens_in, "seq", split_axis=1, concat_axis=0, tiled=True)
    slope_all = lax.all_gather(slope_half, "seq", axis=0, tiled=True)
    first_shard = lax.dot_general(
        columns_all, slope_all, (((0,), (0,)), ((), ())), preferred_element_type=jnp.float32
    )
    output_total, first_bias_total, bias_total, loss_total = lax.psum(
        (second_part, first_bias_part, bias_part, loss_part), ("dp", "seq")
    )
    first_grad = lax.psum(first_shard, "dp")
    first_square = lax.psum(jnp.sum(first_grad * first_grad), "seq")
    step_first = normalized_scores(first_grad, first_square, D * RETAIN_HIDDEN)
    output_weight_step = normalized_scores(
        output_total, jnp.sum(output_total * output_total), RETAIN_HIDDEN * KEY_VALUE_HEADS
    )
    step_bias = normalized_scores(
        first_bias_total, jnp.sum(first_bias_total * first_bias_total), RETAIN_HIDDEN
    )
    return (
        key_attention_mass.reshape(1, KEY_VALUE_HEADS, local_row_slice),
        loss_total,
        step_first,
        output_weight_step,
        step_bias,
        bias_total,
    )


def solution(mesh):
    in_specs = (
        P("dp", "seq", None),
        P("dp", "seq", None),
        P("dp", "seq", None),
        P(),
        P(),
        P(),
        P(),
        P(),
    )
    out_specs = (P("dp", None, "seq"), P(), P("seq", None), P(), P(), P())
    return jax.shard_map(
        per_device, mesh=mesh, in_specs=in_specs, out_specs=out_specs, check_vma=False
    )
```

profile of v0, /device:TPU:1, one launch (start us, length us, event | category | flops | bytes accessed | tf_op | source)
XLA Modules:
  0.0 927.3 jit_solution(2229353486682803280)
XLA Ops:
  11.0 64.1 %all-gather.6.cloned.1.call-done = bf16[1,4096,512]{2,1,0:T(8,128)(2,1)} async-done(((bf16[1,128,512]{2,1,0:T(8,128)(2,1)}), bf16[1,4096,512]{2,1,0:T(8,128)(2,1)}) %all-gather.6.cloned.1.call-update) | async-done | bytes 4194320 | tf_op jit(solution)/shard_map/all_gather | solution.py:108
  75.1 172.1 %while.32 = (s32[]{:T(128)}, f32[4,8,128]{2,1,0:T(8,128)S(1)}, f32[4,8,128]{2,1,0:T(8,128)S(1)}, s32[64]{0:T(128)S(1)}, s32[]{:T(128)}, /*index=5*/s32[128]{0:T(...) while((s32[]{:T(128)}, f32[4,8,128]{2,1,0:T(8,128)S(1)}, ...), condition=%wide.region_9.10_spmd, body=%wide.region_2.9_spmd.sunk | while | flops 68712320 | bytes 3713545 | solution.py:42
  85.6 1.7 conditional.4
  117.8 1.7 conditional.4
  126.1 1.7 conditional.4
  155.0 1.7 conditional.4
  161.1 1.7 conditional.4
  165.1 1.7 conditional.4
  169.0 1.7 conditional.4
  176.8 1.7 conditional.4
  191.8 1.7 conditional.4
  202.3 1.7 conditional.4
  247.3 181.7 %while.33 = (s32[]{:T(128)}, f32[4,4096]{1,0:T(4,128)S(1)}, s32[64]{0:T(128)S(1)}, s32[]{:T(128)}, s32[128]{0:T(128)S(1)}, /*index=5*/bf16[4096,512]{1,0:T(8,128...) while((s32[]{:T(128)}, f32[4,4096]{1,0:T(4,128)S(1)}, ...), condition=%wide.region_16.17_spmd, body=%wide.region_10.16_spmd.sunk | while | flops 68441992 | bytes 1416701 | solution.py:42
  429.0 2.0 copy.51
  431.1 4.8 multiply_convert_fusion
  436.0 231.3 %reduce-scatter.4.cloned.1.call-done = f32[128,4]{1,0:T(8,128)} async-done(((f32[4096,4]{1,0:T(8,128)}), f32[128,4]{1,0:T(8,128)}) %reduce-scatter.4.cloned.1.call-update) | async-done | bytes 2064
  670.0 2.5 copy.42
  672.5 63.8 %all_to_all.19 = bf16[128,32,256]{0,2,1:T(8,128)(2,1)S(1)} all-to-all(bf16[128,32,256]{0,2,1:T(8,128)(2,1)} %bitcast.50), channel_id=1, replica_groups=mesh['dp'=8,'seq'=32] {'seq'}, dimensions={1} | all-to-all | bytes 4194304 | tf_op jit(solution)/shard_map/all_to_all | solution.py:139
  736.3 2.9 copy.43
  739.2 19.6 %all-gather.4.cloned.1.call-done = bf16[4096,512]{1,0:T(8,128)(2,1)} async-done(((bf16[128,512]{1,0:T(8,128)(2,1)}), bf16[4096,512]{1,0:T(8,128)(2,1)}) %all-gather.4.cloned.1.call-update) | async-done | bytes 4194320 | tf_op jit(solution)/shard_map/all_gather | solution.py:140
  758.7 4.9 convolution_bitcast_fusion
  764.5 77.0 %all-reduce = (f32[]{:T(128)}, f32[4,512]{1,0:T(4,128)S(1)}, f32[512]{0:T(512)S(1)}, f32[4]{0:T(128)}) all-reduce(f32[]{:T(128)S(6)} %div.87, f32[4,512]{1,0:T(4,128)S(1)} %fusion.20, f32[512]{0:T(512)S(1)} %get-tuple-element.630, f32[4]{0:T(128)S(1)} %get-tuple-element.583), channel_id=1, replica_groups=mesh['dp'=8,'seq'=32] {'dp','seq'}, use_global_device_ids=true, to_apply=%region_19.20 | all-reduce | flops 2565 | bytes 20520 | tf_op jit(solution)/shard_map/psum | solution.py:144
  844.7 1.8 multiply_reduce_fusion
  847.1 70.8 %psum.44 = f32[]{:T(128)} all-reduce(f32[]{:T(128)} %multiply_reduce_fusion), channel_id=1, replica_groups=mesh['dp'=8,'seq'=32] {'seq'}, use_global_device_ids=true, to_apply=%region_22.23 | all-reduce | flops 1 | bytes 8 | tf_op jit(solution)/shard_map/psum | solution.py:148
  (978 shorter events, 235.0 us)
Async XLA Ops:
  7.2 661.0 %copy-start = (bf16[4,512]{1,0:T(4,128)(2,1)S(1)}, bf16[4,512]{1,0:T(4,128)(2,1)}, u32[]{:S(2)}) copy-start(bf16[4,512]{1,0:T(4,128)(2,1)} %param.22) | copy-start | bytes 12292
  7.2 3.1 copy-start.4
  7.2 67.9 %all-gather.6.cloned.1.call-start = ((), (), s32[]{:S(2)}) async-start(), calls=%async_computation.4 | async-start | bytes 4325376 | tf_op jit(solution)/shard_map/all_gather | solution.py:108
  7.9 659.3 %reduce-scatter.4.cloned.1.call-start = ((), (), s32[]{:S(2)}) async-start(), calls=%async_computation.5 | async-start | bytes 2162688
  429.0 2.1 copy-start.1
  429.0 2.1 copy-start.2
  431.1 237.1 %copy-start.5 = (f32[4]{0:T(128)S(1)}, f32[4]{0:T(128)}, u32[]{:S(2)}) copy-start(f32[4]{0:T(128)} %param.23) | copy-start | bytes 52
  431.1 327.7 %all-gather.4.cloned.1.call-start = ((), (), s32[]{:S(2)}) async-start(), calls=%async_computation.2 | async-start | bytes 4325376 | tf_op jit(solution)/shard_map/all_gather | solution.py:140
  668.1 68.1 %copy-start.3 = (f32[4,128]{1,0:T(4,128)}, f32[4,128]{1,0:T(4,128)S(1)}, u32[]{:S(2)}) copy-start(f32[4,128]{1,0:T(4,128)S(1)} %copy.52) | copy-start | bytes 6148
  669.9 174.8 %all-reduce.3.cloned.1.call-start = ((), (), s32[]{:S(2)}) async-start(), calls=%async_computation.3 | async-start | bytes 1048576 | tf_op jit(solution)/shard_map/psum | solution.py:147
Sparse Core Ops, SparseCore 0:
  10.6 64.5 all-gather.5
  431.2 236.0 reduce-scatter.3
  670.4 88.3 all-gather.3
  763.8 72.7 all-reduce.2
where the time goes:
time: 936 us; the launch traced here: 927 us
  waiting for transfers between devices  316 us (34%)
  blocking collectives  212 us (23%)
  loops' own time  174 us (19%)
  other arithmetic  120 us (13%)
  local copies, waits for them, and re-layouts  57.2 us (6%)
  matrix products  31.2 us (3%)
  between operations  16.7 us (2%)
    unnamed x5, waiting for transfers between devices  232 us
    another operation x2, loops' own time, blockwise(): return lax.fori_loop(0, rows_here // inner, visit_block, carried)  171 us
    psum x1, blocking collectives, per_device(): lax.psum((second_part, first_bias_part, bias_part, loss_part), ('dp', 'se...  77 us
    psum x1, blocking collectives, per_device(): first_square = lax.psum(jnp.sum(first_grad * first_grad), 'seq')  70.8 us
    all_gather x1, waiting for transfers between devices, per_device(): keys_whole = lax.all_gather(local_key_rows, 'seq', axis=0, tiled=True)  64.1 us
    all_to_all x1, blocking collectives, per_device(): lax.all_to_all(tokens_in, 'seq', split_axis=1, concat_axis=0, tiled=True)  63.8 us
    reduce_min x64, other arithmetic, mass_step(): jnp.min(key_pos) > jnp.max(query_pos)  41.8 us
    reduce_min x64, other arithmetic, normalizer_step(): jnp.min(key_pos) > jnp.max(query_pos)  41.8 us
  transfers between devices with their start and end apart: 4, of which 3 were waited for; matrix products, arithmetic and copies ran while one was open for 2% of the time, Pallas kernels for 0%

commit v1 on v0

v1 whole, which is shorter than its diff:
```python
import functools
import math

import jax
import jax.numpy as jnp
from jax import lax
from jax.experimental import pallas as pl
from jax.experimental.pallas import tpu as pltpu
from jax.sharding import PartitionSpec as P

MESH = pl.DeviceIdType.MESH
ROWS = 128
BLK = 64
HEAD_SIZE = 128
KEY_VALUE_HEADS = 4
QUERY_GROUP_SIZE = 8
HIDDEN = 512
KEYS = 512
SCALE2 = HEAD_SIZE**-0.5 * math.log2(math.e)
LAST = (((1,), (1,)), ((), ()))
SEQ_PARTS = (4, 4, 2)


def dot_t(a, b, precision=None):
    return lax.dot_general(a, b, LAST, preferred_element_type=jnp.float32, precision=precision)


def attend(head, order_ref, me, slot_seq, q_buf, k_buf, p_buf, m_buf, mass_out, middle):
    steps = k_buf.shape[1] // KEYS
    width = QUERY_GROUP_SIZE * ROWS
    lane = lax.broadcasted_iota(jnp.int32, (BLK, ROWS), 1)
    low, high = order_ref[2 * me], order_ref[2 * me + 1]
    q_pos = jnp.where(lane < BLK, low, high) * BLK + lax.rem(lane, BLK)
    inner = lax.broadcasted_iota(jnp.int32, (BLK, ROWS), 0)

    def visit(step, carried):
        highest, summed = carried
        first = pl.multiple_of(step * KEYS, KEYS)
        keys = k_buf[head, pl.ds(first, KEYS), :]
        pieces = []
        for part in range(KEYS // BLK):
            owner = slot_seq(step * (KEYS // ROWS) + part // 2)
            k_pos = order_ref[2 * owner + part % 2] * BLK + inner
            pieces.append(jnp.where(k_pos <= q_pos, 0.0, -1e30))
        bias = jnp.concatenate(pieces, axis=0)
        bias = jnp.concatenate([bias, bias], axis=1)
        new_highest, new_summed = [], []
        for pair in range(QUERY_GROUP_SIZE // 2):
            start = pl.multiple_of((head * QUERY_GROUP_SIZE + 2 * pair) * ROWS, 2 * ROWS)
            score = dot_t(keys, q_buf[pl.ds(start, 2 * ROWS), :]) + bias
            old = highest[:, pair * 256 : pair * 256 + 256]
            top = jnp.maximum(old, jnp.max(score, axis=0, keepdims=True))
            weight = jnp.exp2((score - top) * SCALE2)
            total = summed[:, pair * 256 : pair * 256 + 256] * jnp.exp2((old - top) * SCALE2)
            new_highest.append(top)
            new_summed.append(total + jnp.sum(weight, axis=0, keepdims=True))
            p_buf[pl.ds(first, KEYS), pair * 256 : pair * 256 + 256] = weight.astype(jnp.bfloat16)
        highest = jnp.concatenate(new_highest, axis=1)
        m_buf[step, 0:1, :] = highest
        return highest, jnp.concatenate(new_summed, axis=1)

    start_state = (jnp.full((1, width), -1e30, jnp.float32), jnp.zeros((1, width), jnp.float32))
    highest, summed = lax.fori_loop(0, steps, visit, start_state)
    middle()
    inverse = 1.0 / (summed * QUERY_GROUP_SIZE)
    row = lax.broadcasted_iota(jnp.int32, (16, width), 0)

    def collect(step, _):
        first = pl.multiple_of(step * KEYS, KEYS)
        scale = jnp.exp2((m_buf[step, 0:1, :] - highest) * SCALE2) * inverse
        coarse = scale.astype(jnp.bfloat16).astype(jnp.float32)
        both = jnp.where(row == 0, coarse, jnp.where(row == 1, scale - coarse, 0.0))
        mass = dot_t(both.astype(jnp.bfloat16), p_buf[pl.ds(first, KEYS), :])
        line = mass[0:1, :] + mass[1:2, :]
        for part in range(KEYS // ROWS):
            mass_out[step * (KEYS // ROWS) + part, pl.ds(head, 1), :] = line[
                :, part * ROWS : part * ROWS + ROWS
            ]
        return _

    lax.fori_loop(0, steps, collect, 0)


class Gather:
    def __init__(self, view, where, sems):
        self.view, self.where, self.sems = view, where, sems

    def copy(self, block, stage, chunk, hop, device):
        send, recv = self.sems[2 * stage], self.sems[2 * stage + 1]
        place = (chunk, hop)
        return pltpu.make_async_remote_copy(
            src_ref=block,
            dst_ref=block,
            send_sem=send.at[place],
            recv_sem=recv.at[place],
            device_id=device,
            device_id_type=MESH,
        )

    def along_z(self, chunk):
        w = self.where
        return [
            self.copy(
                self.view(chunk, w.slot(w.y, w.z, w.c), 1), 0, chunk, hop,
                w.device(w.y, lax.rem(w.z + hop, w.nz), w.c),
            )
            for hop in range(1, w.nz)
        ]

    def along_y(self, chunk):
        w = self.where
        return [
            self.copy(
                self.view(chunk, w.slot(w.y, 0, w.c), w.nz), 1, chunk, hop,
                w.device(lax.rem(w.y + hop, w.ny), w.z, w.c),
            )
            for hop in range(1, w.ny)
        ]

    def across(self, chunk):
        w = self.where
        return [
            self.copy(
                self.view(chunk, w.slot(0, 0, w.c), w.ny * w.nz), 2, chunk, 0,
                w.device(w.y, w.z, 1 - w.c),
            )
        ]

    def first(self, chunk):
        for copy in self.along_z(chunk):
            copy.start()

    def second(self, chunk):
        w = self.where
        for hop in range(1, w.nz):
            block = self.view(chunk, w.slot(w.y, lax.rem(w.z + w.nz - hop, w.nz), w.c), 1)
            self.copy(block, 0, chunk, hop, w.device(w.y, w.z, 1 - w.c)).wait_recv()
        for copy in self.along_y(chunk):
            copy.start()

    def third(self, chunk):
        w = self.where
        for hop in range(1, w.ny):
            block = self.view(chunk, w.slot(lax.rem(w.y + w.ny - hop, w.ny), 0, w.c), w.nz)
            self.copy(block, 1, chunk, hop, w.device(w.y, w.z, 1 - w.c)).wait_recv()
        for copy in self.across(chunk):
            copy.start()

    def arrive(self, chunk):
        w = self.where
        block = self.view(chunk, w.slot(0, 0, 1 - w.c), w.ny * w.nz)
        self.copy(block, 2, chunk, 0, w.device(w.y, w.z, 1 - w.c)).wait_recv()

    def drain(self, chunk):
        for copy in self.along_z(chunk) + self.along_y(chunk) + self.across(chunk):
            copy.wait_send()


class Where:
    def __init__(self, parts):
        self.ny, self.nz, self.nc = parts
        self.dp, self.seq = lax.axis_index("dp"), lax.axis_index("seq")
        self.c = lax.rem(self.seq, self.nc)
        self.z = lax.rem(self.seq // self.nc, self.nz)
        self.y = self.seq // (self.nc * self.nz)

    def slot(self, y, z, c):
        return (c * self.ny + y) * self.nz + z

    def device(self, y, z, c):
        return (self.dp, (y * self.nz + z) * self.nc + c)

    def slot_seq(self, slot):
        plane = self.ny * self.nz
        return lax.rem(slot, plane) * self.nc + slot // plane

    def seq_slot(self, seq):
        return lax.rem(seq, self.nc) * (self.ny * self.nz) + seq // self.nc


def remote(src, dst, send, recv, device):
    return pltpu.make_async_remote_copy(
        src_ref=src, dst_ref=dst, send_sem=send, recv_sem=recv, device_id=device,
        device_id_type=MESH,
    )


def kernel(
    parts, ndp,
    order_ref, b2_ref, q_hbm, k_hbm, hs_hbm, w1_hbm, b1_ref, w2_ref,
    mass_ref, step_ref, second_ref, first_bias_ref, misc_ref,
    q_buf, k_buf, hs_buf, w1_buf, p_buf, m_buf, cols, s_buf, pre_buf, gate_buf, hid_buf,
    mass_out, mass_in, small_z, small_y, small_c, small_d,
    part_buf, piece_buf, full_buf, sq_seq, sq_dp,
    q_sem, k_sem, hs_sem, w1_sem, own_sem,
    kg0, kg1, kg2, kg3, kg4, kg5, sg0, sg1, sg2, sg3, sg4, sg5,
    a_send, a_recv, m_send, m_recv, z_send, z_recv, y_send, y_recv, c_send, c_recv,
    d_send, d_recv, p_send, p_recv, f_send, f_recv, e_send, e_recv, g_send, g_recv,
):
    w = Where(parts)
    ns = w.ny * w.nz * w.nc
    me, dp = w.seq, w.dp
    mine = w.slot(w.y, w.z, w.c)
    length = float(ns * ROWS)
    depth = hs_hbm.shape[1]
    wide = depth // ns
    height = HIDDEN // ndp
    heads = KEY_VALUE_HEADS

    def key_view(chunk, slot, amount):
        return k_buf.at[chunk, pl.ds(pl.multiple_of(slot * ROWS, ROWS), amount * ROWS), :]

    def slope_view(chunk, slot, amount):
        return s_buf.at[pl.ds(slot, amount), pl.ds(chunk * 128, 128), :]

    key_gather = Gather(key_view, w, (kg0, kg1, kg2, kg3, kg4, kg5))
    slope_gather = Gather(slope_view, w, (sg0, sg1, sg2, sg3, sg4, sg5))

    k_copies = [
        pltpu.make_async_copy(
            k_hbm.at[:, pl.ds(head * HEAD_SIZE, HEAD_SIZE)], key_view(head, mine, 1), k_sem.at[head]
        )
        for head in range(heads)
    ]
    for copy in k_copies:
        copy.start()
    quarters = 4
    span = depth // quarters

    def w1_copy(quarter):
        return pltpu.make_async_copy(
            w1_hbm.at[pl.ds(quarter * span, span), :], w1_buf.at[pl.ds(quarter * span, span), :],
            w1_sem.at[quarter],
        )

    hs_copy = pltpu.make_async_copy(hs_hbm, hs_buf, hs_sem.at[0])
    own_copy = pltpu.make_async_copy(
        hs_hbm.at[:, pl.ds(pl.multiple_of(me * wide, 128), wide)], cols.at[mine], own_sem.at[0]
    )

    def q_copy(head):
        return pltpu.make_async_copy(
            q_hbm.at[:, pl.ds(pl.multiple_of(head * HEAD_SIZE, 128), HEAD_SIZE)],
            q_buf.at[pl.ds(pl.multiple_of(head * ROWS, ROWS), ROWS), :],
            q_sem.at[head],
        )

    hs_copy.start()
    for quarter in range(quarters):
        w1_copy(quarter).start()
    own_copy.start()

    barrier = pltpu.get_barrier_semaphore()

    def greet_seq(hop, _):
        pl.semaphore_signal(
            barrier, inc=1, device_id=(dp, lax.rem(me + hop, ns)), device_id_type=MESH
        )
        return _

    def greet_dp(hop, _):
        pl.semaphore_signal(
            barrier, inc=1, device_id=(lax.rem(dp + hop, ndp), me), device_id_type=MESH
        )
        return _

    lax.fori_loop(1, ns, greet_seq, 0)
    lax.fori_loop(1, ndp, greet_dp, 0)

    def q_start(head, _):
        q_copy(head).start()
        return _

    lax.fori_loop(0, heads * QUERY_GROUP_SIZE, q_start, 0)
    for copy in k_copies:
        copy.wait()
    pl.semaphore_wait(barrier, ns - 1 + ndp - 1)
    for head in range(heads):
        key_gather.first(head)

    hs_copy.wait()
    pre_buf[...] = jnp.broadcast_to(b1_ref[...], (ROWS, HIDDEN))
    for quarter in range(quarters):
        w1_copy(quarter).wait()

        def project(tile, _):
            at = pl.multiple_of(quarter * span + tile * 256, 256)
            pre_buf[...] += jnp.dot(
                hs_buf[:, pl.ds(at, 256)], w1_buf[pl.ds(at, 256), :],
                preferred_element_type=jnp.float32,
            )
            return _

        lax.fori_loop(0, span // 256, project, 0)
        key_gather.second(quarter)

    def a_copy(hop):
        to = lax.rem(me + hop, ns)
        return remote(
            hs_hbm.at[:, pl.ds(pl.multiple_of(to * wide, 128), wide)], cols.at[mine],
            a_send.at[hop], a_recv.at[hop], (dp, to),
        )

    def a_start(hop, _):
        a_copy(hop).start()
        return _

    lax.fori_loop(1, ns, a_start, 0)
    key_gather.third(0)

    pre = jnp.transpose(pre_buf[...])
    gate = 1.0 / (1.0 + jnp.exp(-pre))
    gate_buf[...] = gate * (1.0 + pre * (1.0 - gate))
    hid_buf[...] = (pre * gate).astype(jnp.bfloat16)

    def q_wait(head, _):
        q_copy(head).wait()
        return _

    lax.fori_loop(0, heads * QUERY_GROUP_SIZE, q_wait, 0)

    def one_head(head, _):
        key_gather.arrive(head)

        def middle():
            @pl.when(head < heads - 1)
            def _():
                key_gather.third(head + 1)

        attend(head, order_ref, me, w.slot_seq, q_buf, k_buf, p_buf, m_buf, mass_out, middle)
        return _

    lax.fori_loop(0, heads, one_head, 0)

    def m_copy(hop):
        to = lax.rem(me + hop, ns)
        return remote(
            mass_out.at[w.seq_slot(to)], mass_in.at[hop], m_send.at[hop], m_recv.at[hop], (dp, to)
        )

    def m_start(hop, _):
        m_copy(hop).start()
        return _

    lax.fori_loop(1, ns, m_start, 0)
    predicted = jnp.dot(w2_ref[...], hid_buf[...], preferred_element_type=jnp.float32)
    line = lax.broadcasted_iota(jnp.int32, (heads, ROWS), 0)
    for head in range(heads):
        predicted += jnp.where(line == head, b2_ref[head], 0.0)

    def m_add(hop, total):
        m_copy(hop).wait_recv()
        return total + mass_in[hop]

    mass = lax.fori_loop(1, ns, m_add, mass_out[mine])[0:heads, :]
    mass_ref[...] = mass
    residue = predicted - jnp.log(1.0 + mass)
    out_grad = residue / length
    w2_wide = jnp.concatenate(
        [w2_ref[...].astype(jnp.float32), jnp.zeros((8 - heads, HIDDEN), jnp.float32)], axis=0
    )
    w2_turned = jnp.transpose(w2_wide)
    back = w2_turned[:, 0:1] * out_grad[0:1, :]
    for head in range(1, heads):
        back += w2_turned[:, head : head + 1] * out_grad[head : head + 1, :]
    slope = back * gate_buf[...]
    s_buf[mine] = slope.astype(jnp.bfloat16)
    for chunk in range(4):
        slope_gather.first(chunk)

    def exchange(buf, at, count, send, recv, device):
        return [
            remote(buf.at[at], buf.at[at], send.at[hop], recv.at[hop], device(hop))
            for hop in range(1, count)
        ]

    def z_copies():
        return exchange(
            small_z, w.z, w.nz, z_send, z_recv,
            lambda hop: w.device(w.y, lax.rem(w.z + hop, w.nz), w.c),
        )

    def y_copies():
        return exchange(
            small_y, w.y, w.ny, y_send, y_recv,
            lambda hop: w.device(lax.rem(w.y + hop, w.ny), w.z, w.c),
        )

    def c_copies():
        return exchange(
            small_c, w.c, w.nc, c_send, c_recv, lambda hop: w.device(w.y, w.z, 1 - w.c)
        )

    def d_copies():
        return exchange(
            small_d, dp, ndp, d_send, d_recv, lambda hop: (lax.rem(dp + hop, ndp), me)
        )

    def settle(copies, buf):
        for copy in copies:
            copy.wait_recv()
        total = buf[0]
        for at in range(1, buf.shape[0]):
            total += buf[at]
        return total

    exact = lax.Precision.HIGHEST
    second = dot_t(out_grad, hid_buf[...].astype(jnp.float32), exact)
    ones = jnp.ones((8, ROWS), jnp.float32)
    first_bias = dot_t(ones, slope, exact)[0:1, :]
    place = lax.broadcasted_iota(jnp.int32, (1, HIDDEN), 1)
    bias_sum = jnp.sum(out_grad, axis=1, keepdims=True)
    loss = 0.5 * jnp.sum(jnp.sum(residue * residue, axis=1, keepdims=True), axis=0, keepdims=True)
    last = jnp.where(place == heads, loss / length, 0.0)
    for head in range(heads):
        last = jnp.where(place == head, bias_sum[head : head + 1, :], last)
    small = jnp.concatenate(
        [second, first_bias, last, jnp.zeros((2, HIDDEN), jnp.float32)], axis=0
    )
    small_z[w.z] = small
    for copy in z_copies():
        copy.start()

    for chunk in range(4):
        slope_gather.second(chunk)
    small_y[w.y] = settle(z_copies(), small_z)
    for copy in y_copies():
        copy.start()
    for chunk in range(4):
        slope_gather.third(chunk)
    small_c[w.c] = settle(y_copies(), small_y)
    for copy in c_copies():
        copy.start()

    own_copy.wait()

    def a_wait(hop, _):
        a_copy(hop).wait_recv()
        return _

    lax.fori_loop(1, ns, a_wait, 0)
    small_d[dp] = settle(c_copies(), small_c)
    for copy in d_copies():
        copy.start()

    def p_copy(hop):
        to = lax.rem(dp + hop, ndp)
        return remote(
            part_buf.at[pl.ds(pl.multiple_of(to * height, height), height), :], piece_buf.at[dp],
            p_send.at[hop], p_recv.at[hop], (to, me),
        )

    half = HIDDEN // 2
    for side in range(2):
        rows = pl.ds(side * half, half)
        slope_gather.arrive(2 * side)
        slope_gather.arrive(2 * side + 1)

        def gather_grad(at, total):
            return total + jnp.dot(
                s_buf[at, rows, :], cols[at], preferred_element_type=jnp.float32
            )

        part_buf[rows, :] = lax.fori_loop(
            0, ns, gather_grad, jnp.zeros((half, wide), jnp.float32)
        )
    for hop in range(1, ndp):
        p_copy(hop).start()
    piece_buf[dp] = part_buf[pl.ds(pl.multiple_of(dp * height, height), height), :]
    for hop in range(1, ndp):
        p_copy(hop).wait_recv()
    piece = piece_buf[0]
    for at in range(1, ndp):
        piece += piece_buf[at]
    own_rows = pl.ds(pl.multiple_of(dp * height, height), height)
    full_buf[own_rows, :] = piece

    def f_copy(hop):
        to = lax.rem(dp + hop, ndp)
        return remote(
            full_buf.at[own_rows, :], full_buf.at[own_rows, :], f_send.at[hop], f_recv.at[hop],
            (to, me),
        )

    for hop in range(1, ndp):
        f_copy(hop).start()
    squares = piece * piece
    squares = squares[:, 0:128] + squares[:, 128:256]
    sq_seq[me] = jnp.sum(squares.reshape(height // 8, 8, 128), axis=0)

    def e_copy(hop):
        return remote(
            sq_seq.at[me], sq_seq.at[me], e_send.at[hop], e_recv.at[hop],
            (dp, lax.rem(me + hop, ns)),
        )

    def e_start(hop, _):
        e_copy(hop).start()
        return _

    def e_wait(hop, _):
        e_copy(hop).wait_recv()
        return _

    lax.fori_loop(1, ns, e_start, 0)

    small = settle(d_copies(), small_d)
    second = small[0:heads, :]

    def inverse_root(square_sum, entries):
        return 1.0 / jnp.sqrt(square_sum / entries + 1e-06)

    def whole_sum(x):
        return jnp.sum(jnp.sum(x, axis=1, keepdims=True), axis=0, keepdims=True)

    second_ref[...] = second * inverse_root(whole_sum(second * second), heads * HIDDEN)
    first_bias = small[4:5, :]
    first_bias_ref[...] = first_bias * inverse_root(whole_sum(first_bias * first_bias), HIDDEN)
    misc_ref[...] = small[5:6, 0:128]

    lax.fori_loop(1, ns, e_wait, 0)
    square = sq_seq[0]
    for at in range(1, ns):
        square += sq_seq[at]
    sq_dp[dp] = square

    def g_copy(hop):
        return remote(
            sq_dp.at[dp], sq_dp.at[dp], g_send.at[hop], g_recv.at[hop],
            (lax.rem(dp + hop, ndp), me),
        )

    for hop in range(1, ndp):
        g_copy(hop).start()
    for hop in range(1, ndp):
        f_copy(hop).wait_recv()
    turned = jnp.transpose(full_buf[...])
    for hop in range(1, ndp):
        g_copy(hop).wait_recv()
    square = sq_dp[0]
    for at in range(1, ndp):
        square += sq_dp[at]
    step_ref[...] = turned * inverse_root(whole_sum(square), depth * HIDDEN)

    def drain(hop, _):
        a_copy(hop).wait_send()
        m_copy(hop).wait_send()
        e_copy(hop).wait_send()
        return _

    lax.fori_loop(1, ns, drain, 0)
    for chunk in range(4):
        key_gather.drain(chunk)
        slope_gather.drain(chunk)
    for copy in z_copies() + y_copies() + c_copies() + d_copies():
        copy.wait_send()
    for hop in range(1, ndp):
        p_copy(hop).wait_send()
        f_copy(hop).wait_send()
        g_copy(hop).wait_send()


def per_device(parts, ndp, ns, queries, key_rows, hidden, order, w1, b1, w2, b2):
    f32, bf16 = jnp.float32, jnp.bfloat16
    depth = hidden.shape[2]
    wide = depth // ns
    height = HIDDEN // ndp
    vmem, smem, anywhere = (
        pl.BlockSpec(memory_space=pltpu.VMEM),
        pl.BlockSpec(memory_space=pltpu.SMEM),
        pl.BlockSpec(memory_space=pl.ANY),
    )
    ny, nz, nc = parts
    dma = pltpu.SemaphoreType.DMA
    gather_sems = [dma((4, n)) for n in (nz, nz, ny, ny, 1, 1)]
    heads = KEY_VALUE_HEADS
    mass, step, second, first_bias, misc = pl.pallas_call(
        functools.partial(kernel, parts, ndp),
        out_shape=(
            jax.ShapeDtypeStruct((heads, ROWS), f32),
            jax.ShapeDtypeStruct((wide, HIDDEN), f32),
            jax.ShapeDtypeStruct((heads, HIDDEN), f32),
            jax.ShapeDtypeStruct((1, HIDDEN), f32),
            jax.ShapeDtypeStruct((1, 128), f32),
        ),
        in_specs=[smem, smem, anywhere, anywhere, anywhere, anywhere, vmem, vmem],
        out_specs=(vmem,) * 5,
        scratch_shapes=[
            pltpu.VMEM((heads * QUERY_GROUP_SIZE * ROWS, HEAD_SIZE), bf16),
            pltpu.VMEM((heads, ns * ROWS, HEAD_SIZE), bf16),
            pltpu.VMEM((ROWS, depth), bf16),
            pltpu.VMEM((depth, HIDDEN), bf16),
            pltpu.VMEM((ns * ROWS, QUERY_GROUP_SIZE * ROWS), bf16),
            pltpu.VMEM((ns * ROWS // KEYS, 8, QUERY_GROUP_SIZE * ROWS), f32),
            pltpu.VMEM((ns, ROWS, wide), bf16),
            pltpu.VMEM((ns, HIDDEN, ROWS), bf16),
            pltpu.VMEM((ROWS, HIDDEN), f32),
            pltpu.VMEM((HIDDEN, ROWS), f32),
            pltpu.VMEM((HIDDEN, ROWS), bf16),
            pltpu.VMEM((ns, 8, ROWS), f32),
            pltpu.VMEM((ns, 8, ROWS), f32),
            pltpu.VMEM((nz, 8, HIDDEN), f32),
            pltpu.VMEM((ny, 8, HIDDEN), f32),
            pltpu.VMEM((nc, 8, HIDDEN), f32),
            pltpu.VMEM((ndp, 8, HIDDEN), f32),
            pltpu.VMEM((HIDDEN, wide), f32),
            pltpu.VMEM((ndp, height, wide), f32),
            pltpu.VMEM((HIDDEN, wide), f32),
            pltpu.VMEM((ns, 8, 128), f32),
            pltpu.VMEM((ndp, 8, 128), f32),
            dma((heads * QUERY_GROUP_SIZE,)), dma((4,)), dma((1,)), dma((4,)), dma((1,)),
            *gather_sems, *gather_sems,
            dma((ns,)), dma((ns,)), dma((ns,)), dma((ns,)),
            dma((nz,)), dma((nz,)), dma((ny,)), dma((ny,)), dma((nc,)), dma((nc,)),
            dma((ndp,)), dma((ndp,)), dma((ndp,)), dma((ndp,)), dma((ndp,)), dma((ndp,)),
            dma((ns,)), dma((ns,)), dma((ndp,)), dma((ndp,)),
        ],
        compiler_params=pltpu.CompilerParams(
            collective_id=0, has_side_effects=True, vmem_limit_bytes=60 * 1024 * 1024
        ),
    )(
        order, b2, queries.reshape(ROWS, -1), key_rows.reshape(ROWS, -1),
        hidden.reshape(ROWS, depth), w1, b1.reshape(1, HIDDEN), w2,
    )
    return (
        mass.reshape(1, heads, ROWS), misc[0, heads], step, second, first_bias.reshape(HIDDEN),
        misc[0, 0:heads],
    )


def solution(mesh, parts=SEQ_PARTS):
    in_specs = (P("dp", "seq", None),) * 3 + (P(),) * 5
    out_specs = (P("dp", None, "seq"), P(), P("seq", None), P(), P(), P())
    body = functools.partial(per_device, parts, mesh.shape["dp"], mesh.shape["seq"])
    return jax.shard_map(
        body, mesh=mesh, in_specs=in_specs, out_specs=out_specs, check_vma=False
    )
```

time: 936 us -> 174 us (0.19)
  waiting for transfers between devices: 316 us -> 0 us
  blocking collectives: 212 us -> 0 us
  loops' own time: 174 us -> 0 us
  Pallas kernels: 0 us -> 165 us
  other arithmetic: 120 us -> 0 us
  local copies, waits for them, and re-layouts: 57.2 us -> 7.93 us
  matrix products: 31.2 us -> 0 us
  between operations: 16.7 us -> 0.65 us
    unnamed x5 -> x0, waiting for transfers between devices: 232 us -> none
    another operation x130 -> x0, loops' own time: 174 us -> none  [the longest x2 171 us: blockwise(): return lax.fori_loop(0, rows_here // inner, visit_block, carried)]
    pallas_call x0 -> x1, Pallas kernels: none -> 165 us  [per_device(): pl.pallas_call(functools.partial(kernel, parts, ndp), out_shape=(jax.Shap...]
    psum x2 -> x0, blocking collectives: 148 us -> none  [the longest x1 77 us: per_device(): lax.psum((second_part, first_bias_part, bias_part, loss_part), ('dp', 'se...]
    all_gather x2 -> x0, waiting for transfers between devices: 83.7 us -> none  [the longest x1 64.1 us: per_device(): keys_whole = lax.all_gather(local_key_rows, 'seq', axis=0, tiled=True)]
    reduce_min x128 -> x0, other arithmetic: 83.5 us -> none  [the longest x64 41.8 us: mass_step(): jnp.min(key_pos) > jnp.max(query_pos)]
    all_to_all x1 -> x0, blocking collectives: 63.8 us -> none  [per_device(): lax.all_to_all(tokens_in, 'seq', split_axis=1, concat_axis=0, tiled=True)]
    dot_general x41 -> x0, matrix products: 31.2 us -> none  [the longest x36 19.5 us: raw_scores(): jnp.einsum('tkgd,nkd->kgtn', head_queries, head_keys, preferred_element_t...]
  transfers between devices with their start and end apart: 4 -> 0, of which waited for: 3 -> 0; matrix products, arithmetic and copies ran while one was open for 2% -> 0% of each run, Pallas kernels for 0% -> 0%
where the time goes in v1:
time: 174 us; the launch traced here: 173 us
  Pallas kernels  165 us (95%)
  local copies, waits for them, and re-layouts  7.93 us (5%)
    pallas_call x1, Pallas kernels, per_device(): pl.pallas_call(functools.partial(kernel, parts, ndp), out_shape=(jax.Shap...  165 us
    unnamed x4, local copies, waits for them, and re-layouts  5.65 us

profile of v1, /device:TPU:1, one launch (start us, length us, event | category | flops | bytes accessed | tf_op | source)
XLA Modules:
  0.0 173.2 jit_solution(2368027206304239352)
XLA Ops:
  0.6 164.7 %shard_map.127 = (f32[4,128]{1,0:T(4,128)}, f32[256,512]{1,0:T(8,128)}, f32[4,512]{1,0:T(4,128)}, f32[1,512]{1,0:T(1,128)}, f32[1,128]{1,0:T(1,128)}) custom-call(s32[64]{0:T(128)} %order_ref.1, f32[4]{0:T(128)} %b2_ref.1, bf16[128,4096]{1,0:T(8,128)(2,1)} %bitcast.10, bf16[128,512]{1,0:T(8,128)(2,1)} %bitcast.11, bf16[128,8192]{1,0:T(8,128)(2,1)} %bitcast.9, ...), custom_call_target="tpu_custom_call" | custom-call | tf_op jit(solution)/shard_map/pallas_call | solution.py:577
  165.3 1.2 slice.6
  166.5 1.1 slice_bitcast_fusion
  167.6 1.2 copy.18
  168.8 1.9 %copy.19 = f32[256,512]{1,0:T(8,128)} copy(f32[256,512]{1,0:T(8,128)} %get-tuple-element.24) | data formatting | bytes 1048576
  170.7 1.3 copy.20
  172.0 1.2 copy.21

commit v2 on v0

v2 whole, which is shorter than its diff:
```python
import functools
import math

import jax
import jax.numpy as jnp
from jax import lax
from jax.experimental import pallas as pl
from jax.experimental.pallas import tpu as pltpu
from jax.sharding import PartitionSpec as P

MESH = pl.DeviceIdType.MESH
ROWS = 128
BLK = 64
HEAD_SIZE = 128
HEADS = 4
GROUP = 8
HIDDEN = 512
KEYS = 512
CHUNKS = 4
SCALE2 = HEAD_SIZE**-0.5 * math.log2(math.e)
LAST = (((1,), (1,)), ((), ()))
DP_PARTS = (2, 4)
SEQ_PARTS = (4, 4, 2)


def dot_t(a, b, precision=None):
    return lax.dot_general(a, b, LAST, preferred_element_type=jnp.float32, precision=precision)


def dot(a, b, precision=None):
    return jnp.dot(a, b, preferred_element_type=jnp.float32, precision=precision)


def ring(at, hop, size):
    return lax.rem(at + hop, size)


def remote(src, dst, send, recv, device):
    return pltpu.make_async_remote_copy(
        src_ref=src, dst_ref=dst, send_sem=send, recv_sem=recv, device_id=device,
        device_id_type=MESH,
    )


class Where:
    def __init__(self, dp_parts, seq_parts):
        self.nl, self.nx = dp_parts
        self.ny, self.nz, self.nc = seq_parts
        self.dp, self.seq = lax.axis_index("dp"), lax.axis_index("seq")
        self.x, self.l = lax.rem(self.dp, self.nx), self.dp // self.nx
        self.c = lax.rem(self.seq, self.nc)
        self.z = lax.rem(self.seq // self.nc, self.nz)
        self.y = self.seq // (self.nc * self.nz)

    def device(self, x=None, y=None, z=None, l=None, c=None):
        x, y, z, l, c = (
            own if given is None else given
            for given, own in zip((x, y, z, l, c), (self.x, self.y, self.z, self.l, self.c))
        )
        return (l * self.nx + x, (y * self.nz + z) * self.nc + c)


class Gather:
    def __init__(self, w, axis, view, y_first, sems):
        self.w, self.axis, self.view, self.sems, self.y_first = w, axis, view, sems, y_first
        self.b, self.nb = (w.z, w.nz) if axis == "z" else (w.x, w.nx)

    def copy(self, block, stage, chunk, hop, device):
        place = (chunk, hop)
        return remote(
            block, block, self.sems[2 * stage].at[place], self.sems[2 * stage + 1].at[place], device
        )

    def sent(self, chunk, stage):
        w = self.w
        y_step = stage == (0 if chunk in self.y_first else 1)
        if stage == 2:
            return [(self.view(chunk, w.c), 0, w.device(c=1 - w.c))]
        if stage == 0:
            block = self.view(chunk, w.c, w.y, self.b)
        elif y_step:
            block = self.view(chunk, w.c, w.y)
        else:
            block = self.view(chunk, w.c, slice(None), self.b)
        if y_step:
            return [(block, hop, w.device(y=ring(w.y, hop, w.ny))) for hop in range(1, w.ny)]
        return [
            (block, hop, w.device(**{self.axis: ring(self.b, hop, self.nb)}))
            for hop in range(1, self.nb)
        ]

    def received(self, chunk, stage):
        w = self.w
        y_step = stage == (0 if chunk in self.y_first else 1)
        if stage == 2:
            return [(self.view(chunk, 1 - w.c), 0)]
        result = []
        for hop in range(1, w.ny if y_step else self.nb):
            if y_step:
                at_y, at_b = ring(w.y, w.ny - hop, w.ny), self.b
            else:
                at_y, at_b = w.y, ring(self.b, self.nb - hop, self.nb)
            if stage == 0:
                block = self.view(chunk, w.c, at_y, at_b)
            elif y_step:
                block = self.view(chunk, w.c, at_y)
            else:
                block = self.view(chunk, w.c, slice(None), at_b)
            result.append((block, hop))
        return result

    def start(self, chunk, stage):
        for block, hop, device in self.sent(chunk, stage):
            self.copy(block, stage, chunk, hop, device).start()

    def arrive(self, chunk, stage):
        for block, hop in self.received(chunk, stage):
            self.copy(block, stage, chunk, hop, self.w.device(c=1 - self.w.c)).wait_recv()

    def forward(self, chunk, stage):
        self.arrive(chunk, stage - 1)
        self.start(chunk, stage)

    def drain(self, chunk):
        for stage in range(3):
            for block, hop, device in self.sent(chunk, stage):
                self.copy(block, stage, chunk, hop, device).wait_send()


def attend(head, order_ref, w, q_buf, k_buf, p_buf, m_buf, mass_out, before, middle):
    steps = w.nc * w.ny
    keys_here = w.nz * ROWS
    width = GROUP * ROWS
    lane = lax.broadcasted_iota(jnp.int32, (BLK, ROWS), 1)
    low, high = order_ref[2 * w.seq], order_ref[2 * w.seq + 1]
    q_pos = jnp.where(lane < BLK, low, high) * BLK + lax.rem(lane, BLK)
    inner = lax.broadcasted_iota(jnp.int32, (BLK, ROWS), 0)

    def visit(step, carried):
        before(step)
        highest, summed = carried
        c, y = lax.rem(w.c + step // w.ny, w.nc), lax.rem(w.y + step, w.ny)
        keys = k_buf[head, c, y].reshape(keys_here, HEAD_SIZE)
        pieces = []
        for part in range(keys_here // BLK):
            owner = (y * w.nz + part // 2) * w.nc + c
            k_pos = order_ref[2 * owner + part % 2] * BLK + inner
            pieces.append(jnp.where(k_pos <= q_pos, 0.0, -1e30))
        bias = jnp.concatenate(pieces, axis=0)
        bias = jnp.concatenate([bias, bias], axis=1)
        new_highest, new_summed = [], []
        for pair in range(GROUP // 2):
            start = pl.multiple_of((head * GROUP + 2 * pair) * ROWS, 2 * ROWS)
            score = dot_t(keys, q_buf[pl.ds(start, 2 * ROWS), :]) + bias
            old = highest[:, pair * 256 : pair * 256 + 256]
            top = jnp.maximum(old, jnp.max(score, axis=0, keepdims=True))
            weight = jnp.exp2((score - top) * SCALE2)
            total = summed[:, pair * 256 : pair * 256 + 256] * jnp.exp2((old - top) * SCALE2)
            new_highest.append(top)
            new_summed.append(total + jnp.sum(weight, axis=0, keepdims=True))
            p_buf[step, :, pair * 256 : pair * 256 + 256] = weight.astype(jnp.bfloat16)
        highest = jnp.concatenate(new_highest, axis=1)
        m_buf[step, 0:1, :] = highest
        return highest, jnp.concatenate(new_summed, axis=1)

    start_state = (jnp.full((1, width), -1e30, jnp.float32), jnp.zeros((1, width), jnp.float32))
    highest, summed = lax.fori_loop(0, steps, visit, start_state)
    middle()
    inverse = 1.0 / (summed * GROUP)
    row = lax.broadcasted_iota(jnp.int32, (16, width), 0)

    def collect(step, _):
        scale = jnp.exp2((m_buf[step, 0:1, :] - highest) * SCALE2) * inverse
        coarse = scale.astype(jnp.bfloat16).astype(jnp.float32)
        both = jnp.where(row == 0, coarse, jnp.where(row == 1, scale - coarse, 0.0))
        mass = dot_t(both.astype(jnp.bfloat16), p_buf[step])
        line = mass[0:1, :] + mass[1:2, :]
        c, y = lax.rem(w.c + step // w.ny, w.nc), lax.rem(w.y + step, w.ny)
        for part in range(w.nz):
            mass_out[(y * w.nz + part) * w.nc + c, pl.ds(head, 1), :] = line[
                :, part * ROWS : part * ROWS + ROWS
            ]
        return _

    lax.fori_loop(0, steps, collect, 0)


def inverse_root(square_sum, entries):
    return 1.0 / jnp.sqrt(square_sum / entries + 1e-06)


def whole_sum(x):
    return jnp.sum(jnp.sum(x, axis=1, keepdims=True), axis=0, keepdims=True)


def kernel(
    dp_parts, seq_parts,
    order_ref, b2_ref, q_hbm, k_hbm, hs_hbm, w1_hbm, b1_ref, w2_ref,
    step_ref, small_ref,
    q_buf, k_buf, hs_buf, turned, w1_buf, p_buf, m_buf, cols, s_buf, pre_buf, gate_buf, hid_buf,
    mass_out, mass_in, small_z, small_y, small_c, small_d,
    part_buf, piece_buf, full_buf, sq_seq, sq_dp,
    q_sem, k_sem, hs_sem, w1_sem,
    kg0, kg1, kg2, kg3, kg4, kg5, sg0, sg1, sg2, sg3, sg4, sg5,
    a_send, a_recv, m_send, m_recv, z_send, z_recv, y_send, y_recv, c_send, c_recv,
    d_send, d_recv, p_send, p_recv, f_send, f_recv, e_send, e_recv, g_send, g_recv,
):
    w = Where(dp_parts, seq_parts)
    ns, ndp, plane = w.ny * w.nz * w.nc, w.nl * w.nx, w.nc * w.ny * w.nx
    me, dp = w.seq, w.dp
    length = float(ns * ROWS)
    depth = hs_hbm.shape[1]
    wide = depth // ns
    sub = wide // w.nx
    side_width = HIDDEN // w.nl

    def key_view(chunk, *at):
        return k_buf.at[(chunk, *at)]

    def slope_view(chunk, *at):
        at = at + (slice(None),) * (4 - len(at))
        return s_buf.at[(*at, pl.ds(chunk * 128, 128))]

    key_gather = Gather(w, "z", key_view, (), (kg0, kg1, kg2, kg3, kg4, kg5))
    slope_gather = Gather(w, "x", slope_view, (1, 3), (sg0, sg1, sg2, sg3, sg4, sg5))

    k_copies = [
        pltpu.make_async_copy(
            k_hbm.at[:, pl.ds(head * HEAD_SIZE, HEAD_SIZE)], key_view(head, w.c, w.y, w.z),
            k_sem.at[head],
        )
        for head in range(HEADS)
    ]
    for copy in k_copies:
        copy.start()

    barrier = pltpu.get_barrier_semaphore()

    def greet(device):
        pl.semaphore_signal(barrier, inc=1, device_id=device, device_id_type=MESH)

    def greet_seq(hop, _):
        greet((dp, ring(me, hop, ns)))
        return _

    def in_plane(index):
        return lax.rem(index, w.nx), lax.rem(index // w.nx, w.ny), index // (w.nx * w.ny)

    own_plane = (w.c * w.ny + w.y) * w.nx + w.x

    def plane_device(hop):
        x, y, c = in_plane(ring(own_plane, hop, plane))
        return w.device(x=x, y=y, c=c)

    def greet_plane(hop, _):
        greet(plane_device(hop))
        return _

    def greet_dp(hop, _):
        greet((ring(dp, hop, ndp), me))
        return _

    own_column = w.z * w.nl + w.l
    column = w.nz * w.nl

    def greet_column(hop, _):
        at = ring(own_column, hop, column)
        greet(w.device(z=at // w.nl, l=lax.rem(at, w.nl)))
        return _

    lax.fori_loop(1, ns, greet_seq, 0)
    lax.fori_loop(1, plane, greet_plane, 0)
    lax.fori_loop(1, ndp, greet_dp, 0)
    lax.fori_loop(1, column, greet_column, 0)

    quarters = CHUNKS
    span = depth // quarters

    def w1_copy(quarter):
        return pltpu.make_async_copy(
            w1_hbm.at[pl.ds(quarter * span, span), :], w1_buf.at[pl.ds(quarter * span, span), :],
            w1_sem.at[quarter],
        )

    hs_copy = pltpu.make_async_copy(hs_hbm, hs_buf, hs_sem.at[0])
    hs_copy.start()
    for quarter in range(quarters):
        w1_copy(quarter).start()

    def q_copy(head):
        return pltpu.make_async_copy(
            q_hbm.at[:, pl.ds(pl.multiple_of(head * HEAD_SIZE, 128), HEAD_SIZE)],
            q_buf.at[pl.ds(pl.multiple_of(head * ROWS, ROWS), ROWS), :],
            q_sem.at[head],
        )

    def q_start(head, _):
        q_copy(head).start()
        return _

    lax.fori_loop(0, HEADS * GROUP, q_start, 0)

    tiles = 128 // math.gcd(sub, 128)
    rows_of = min(sub, 128)

    def turn(tile, _):
        value = jnp.transpose(hs_buf[:, pl.ds(pl.multiple_of(tile * 128, 128), 128)])
        block, inside = tile // (wide // 128), lax.rem(tile, wide // 128)
        c = lax.rem(block, w.nc)
        z = lax.rem(block // w.nc, w.nz)
        y = block // (w.nc * w.nz)
        if sub <= 128:
            turned[y, z, c, pl.ds(inside * tiles, tiles)] = value.reshape(tiles, rows_of, ROWS)
        else:
            per = sub // 128
            start = pl.multiple_of(lax.rem(inside, per) * 128, 128)
            turned[y, z, c, inside // per, pl.ds(start, 128), :] = value
        return _

    for copy in k_copies:
        copy.wait()
    pl.semaphore_wait(barrier, ns - 1 + plane - 1 + ndp - 1 + column - 1)
    for head in range(HEADS):
        key_gather.start(head, 0)
    hs_copy.wait()

    pre_buf[...] = jnp.broadcast_to(b1_ref[...], (ROWS, HIDDEN))
    per_quarter = depth // 128 // quarters
    deep = min(1024, span)
    for quarter in range(quarters):
        w1_copy(quarter).wait()

        def project(tile, _):
            at = pl.multiple_of(quarter * span + tile * deep, deep)
            pre_buf[...] += dot(hs_buf[:, pl.ds(at, deep)], w1_buf[pl.ds(at, deep), :])
            return _

        lax.fori_loop(0, span // deep, project, 0)
        lax.fori_loop(quarter * per_quarter, (quarter + 1) * per_quarter, turn, 0)
        if quarter:
            key_gather.forward(quarter - 1, 1)
    key_gather.forward(CHUNKS - 1, 1)

    pre = pre_buf[...]
    gate = 1.0 / (1.0 + jnp.exp(-pre))
    gate_buf[...] = gate * (1.0 + pre * (1.0 - gate))
    hid_buf[...] = (pre * gate).astype(jnp.bfloat16)

    own_cols = cols.at[:, :, pl.ds(pl.multiple_of(own_plane * ROWS, ROWS), ROWS)]

    def a_copy(hop):
        x, y, c = in_plane(ring(own_plane, hop, plane))
        return remote(
            turned.at[y, :, c, x], own_cols, a_send.at[hop], a_recv.at[hop],
            w.device(x=x, y=y, c=c),
        )

    def a_start(hop, _):
        a_copy(hop).start()
        return _

    def q_wait(head, _):
        q_copy(head).wait()
        return _

    lax.fori_loop(0, HEADS * GROUP, q_wait, 0)
    cols[:, :, pl.ds(pl.multiple_of(own_plane * ROWS, ROWS), ROWS)] = turned[w.y, :, w.c, w.x]

    def one_head(head, _):
        def before(step):
            @pl.when((head == 0) & (step == 1))
            def _():
                key_gather.forward(0, 2)

            @pl.when(step == w.ny)
            def _():
                key_gather.arrive(head, 2)

        def middle():
            @pl.when(head < HEADS - 1)
            def _():
                key_gather.forward(head + 1, 2)

            @pl.when(head == 1)
            def _():
                lax.fori_loop(1, plane, a_start, 0)

        attend(head, order_ref, w, q_buf, k_buf, p_buf, m_buf, mass_out, before, middle)
        return _

    lax.fori_loop(0, HEADS, one_head, 0)

    def m_copy(hop):
        to = ring(me, hop, ns)
        return remote(mass_out.at[to], mass_in.at[hop], m_send.at[hop], m_recv.at[hop], (dp, to))

    def m_start(hop, _):
        m_copy(hop).start()
        return _

    lax.fori_loop(1, ns, m_start, 0)
    predicted = dot_t(w2_ref[...], hid_buf[...])
    line = lax.broadcasted_iota(jnp.int32, (HEADS, ROWS), 0)
    for head in range(HEADS):
        predicted += jnp.where(line == head, b2_ref[head], 0.0)

    for chunk in range(CHUNKS):
        key_gather.drain(chunk)

    def m_add(hop, total):
        m_copy(hop).wait_recv()
        return total + mass_in[hop]

    mass = lax.fori_loop(1, ns, m_add, mass_out[me])
    residue = predicted - jnp.log(1.0 + mass)
    out_grad = residue / length
    turned_grad = jnp.transpose(
        jnp.concatenate([out_grad, jnp.zeros((8 - HEADS, ROWS), jnp.float32)], axis=0)
    )
    w2_wide = w2_ref[...].astype(jnp.float32)
    back = turned_grad[:, 0:1] * w2_wide[0:1, :]
    for head in range(1, HEADS):
        back += turned_grad[:, head : head + 1] * w2_wide[head : head + 1, :]
    slope = back * gate_buf[...]
    s_buf[w.c, w.y, w.x] = slope.astype(jnp.bfloat16)
    for chunk in range(CHUNKS):
        slope_gather.start(chunk, 0)

    def exchange(buf, at, count, send, recv, device):
        return [
            remote(buf.at[at], buf.at[at], send.at[hop], recv.at[hop], device(hop))
            for hop in range(1, count)
        ]

    def z_copies():
        return exchange(
            small_z, w.z, w.nz, z_send, z_recv, lambda hop: w.device(z=ring(w.z, hop, w.nz))
        )

    def y_copies():
        return exchange(
            small_y, w.y, w.ny, y_send, y_recv, lambda hop: w.device(y=ring(w.y, hop, w.ny))
        )

    def c_copies():
        return exchange(small_c, w.c, w.nc, c_send, c_recv, lambda hop: w.device(c=1 - w.c))

    def d_copies():
        return exchange(small_d, dp, ndp, d_send, d_recv, lambda hop: (ring(dp, hop, ndp), me))

    def settle(copies, buf):
        for copy in copies:
            copy.wait_recv()
        total = buf[0]
        for at in range(1, buf.shape[0]):
            total += buf[at]
        return total

    exact = lax.Precision.HIGHEST
    second = dot(out_grad, hid_buf[...].astype(jnp.float32), exact)
    first_bias = jnp.sum(slope, axis=0, keepdims=True)
    place = lax.broadcasted_iota(jnp.int32, (1, HIDDEN), 1)
    bias_sum = jnp.sum(out_grad, axis=1, keepdims=True)
    loss = 0.5 * whole_sum(residue * residue)
    last = jnp.where(place == HEADS, loss / length, 0.0)
    for head in range(HEADS):
        last = jnp.where(place == head, bias_sum[head : head + 1, :], last)
    small_z[w.z] = jnp.concatenate(
        [second, first_bias, last, jnp.zeros((2, HIDDEN), jnp.float32)], axis=0
    )
    for copy in z_copies():
        copy.start()

    def m_drain(hop, _):
        m_copy(hop).wait_send()
        return _

    lax.fori_loop(1, ns, m_drain, 0)
    for chunk in range(CHUNKS):
        slope_gather.forward(chunk, 1)
    small_y[w.y] = settle(z_copies(), small_z)
    for copy in y_copies():
        copy.start()
    slope_gather.forward(0, 2)
    slope_gather.forward(1, 2)

    def a_wait(hop, _):
        a_copy(hop).wait()
        return _

    lax.fori_loop(1, plane, a_wait, 0)

    def p_copy(side, hop):
        to = ring(w.z, hop, w.nz)
        return remote(
            part_buf.at[side, to], piece_buf.at[own_column],
            p_send.at[side * w.nz + hop], p_recv.at[w.l * w.nz + hop], w.device(z=to, l=side),
        )

    def each_piece(side, action):
        for hop in range(w.nz):
            if hop:
                action(hop)
            else:
                pl.when(w.l != side)(functools.partial(action, hop))

    for side in range(w.nl):
        chunks = range(side * CHUNKS // w.nl, (side + 1) * CHUNKS // w.nl)
        for chunk in chunks:
            slope_gather.arrive(chunk, 2)
        if side == 0:
            for chunk in range(2, CHUNKS):
                slope_gather.forward(chunk, 2)
            if w.nl == 1:
                for chunk in range(2, CHUNKS):
                    slope_gather.arrive(chunk, 2)
        columns = pl.ds(side * side_width, side_width)
        total = dot(
            cols[...].reshape(w.nz * sub, plane * ROWS),
            s_buf[:, :, :, :, columns].reshape(plane * ROWS, side_width),
        )
        part_buf[side] = total.reshape(w.nz, sub, side_width)
        each_piece(side, lambda hop, side=side: p_copy(side, hop).start())
        if side == 0:
            small_c[w.c] = settle(y_copies(), small_y)
            for copy in c_copies():
                copy.start()

    small_d[dp] = settle(c_copies(), small_c)
    for copy in d_copies():
        copy.start()
    piece_buf[own_column] = part_buf[w.l, w.z]
    for chunk in range(CHUNKS):
        slope_gather.drain(chunk)
    for copy in z_copies() + y_copies() + c_copies():
        copy.wait_send()

    def p_wait(other, hop):
        at = ring(w.z, w.nz - hop, w.nz) * w.nl + other
        remote(
            piece_buf.at[at], piece_buf.at[at], p_send.at[other * w.nz + hop],
            p_recv.at[other * w.nz + hop], w.device(c=1 - w.c),
        ).wait_recv()

    for other in range(w.nl):
        each_piece(other, lambda hop, other=other: p_wait(other, hop))
    piece = piece_buf[0]
    for at in range(1, column):
        piece += piece_buf[at]
    squares = piece * piece
    narrow = squares[:, 0:128]
    for at in range(1, side_width // 128):
        narrow += squares[:, at * 128 : at * 128 + 128]
    sq_seq[me] = jnp.sum(narrow, axis=0, keepdims=True)

    def e_copy(hop):
        return remote(
            sq_seq.at[me], sq_seq.at[me], e_send.at[hop], e_recv.at[hop], (dp, ring(me, hop, ns))
        )

    def e_start(hop, _):
        e_copy(hop).start()
        return _

    def e_wait(hop, _):
        e_copy(hop).wait_recv()
        return _

    lax.fori_loop(1, ns, e_start, 0)
    full_buf[w.l, w.x] = piece

    def f_copy(hop):
        own = full_buf.at[w.l, w.x]
        return remote(own, own, f_send.at[hop], f_recv.at[hop], (ring(dp, hop, ndp), me))

    for hop in range(1, ndp):
        f_copy(hop).start()

    small = settle(d_copies(), small_d)
    second = small[0:HEADS, :]
    small_ref[0:HEADS, :] = second * inverse_root(whole_sum(second * second), HEADS * HIDDEN)
    first_bias = small[4:5, :]
    small_ref[4:5, :] = first_bias * inverse_root(whole_sum(first_bias * first_bias), HIDDEN)
    small_ref[5:6, :] = small[5:6, :]
    small_ref[8 : 8 + HEADS, 0:ROWS] = mass

    for side in range(w.nl):
        each_piece(side, lambda hop, side=side: p_copy(side, hop).wait_send())
    lax.fori_loop(1, ns, e_wait, 0)
    square = sq_seq[0]
    for at in range(1, ns):
        square += sq_seq[at]
    sq_dp[dp] = square

    def g_copy(hop):
        return remote(
            sq_dp.at[dp], sq_dp.at[dp], g_send.at[hop], g_recv.at[hop], (ring(dp, hop, ndp), me)
        )

    for hop in range(1, ndp):
        g_copy(hop).start()
    for hop in range(1, ndp):
        f_copy(hop).wait_recv()
    for hop in range(1, ndp):
        g_copy(hop).wait_recv()
    square = sq_dp[0]
    for at in range(1, ndp):
        square += sq_dp[at]
    scale = inverse_root(whole_sum(square), depth * HIDDEN)
    for side in range(w.nl):
        step_ref[:, side * side_width : (side + 1) * side_width] = (
            full_buf[side].reshape(wide, side_width) * scale
        )

    def e_drain(hop, _):
        e_copy(hop).wait_send()
        return _

    lax.fori_loop(1, ns, e_drain, 0)
    for copy in d_copies():
        copy.wait_send()
    for hop in range(1, ndp):
        f_copy(hop).wait_send()
        g_copy(hop).wait_send()


def finish(step_in, small_in, mass_ref, loss_ref, step_ref, second_ref, first_bias_ref, bias_ref):
    step_ref[...] = step_in[...]
    mass_ref[0] = small_in[8 : 8 + HEADS, 0:ROWS]
    loss_ref[...] = small_in[5:6, HEADS : HEADS + 1]
    second_ref[...] = small_in[0:HEADS, :]
    first_bias_ref[...] = small_in[4:5, :]
    bias_ref[...] = small_in[5:6, 0:HEADS]


def per_device(
    dp_parts, seq_parts, queries, key_rows, hidden, order, w1, b1, w2, b2
):
    f32, bf16 = jnp.float32, jnp.bfloat16
    (nl, nx), (ny, nz, nc) = dp_parts, seq_parts
    ns, ndp, plane, column = ny * nz * nc, nl * nx, nc * ny * nx, nz * nl
    depth = hidden.shape[2]
    wide = depth // ns
    sub, side_width = wide // nx, HIDDEN // nl
    vmem, smem, anywhere = (
        pl.BlockSpec(memory_space=pltpu.VMEM),
        pl.BlockSpec(memory_space=pltpu.SMEM),
        pl.BlockSpec(memory_space=pl.ANY),
    )
    dma = pltpu.SemaphoreType.DMA
    key_sems = [dma((CHUNKS, n)) for n in (nz, nz, ny, ny, 1, 1)]
    slope_sems = [dma((CHUNKS, max(nx, ny)))] * 4 + [dma((CHUNKS, 1))] * 2
    step, small = pl.pallas_call(
        functools.partial(kernel, dp_parts, seq_parts),
        out_shape=(
            jax.ShapeDtypeStruct((wide, HIDDEN), f32),
            jax.ShapeDtypeStruct((16, HIDDEN), f32),
        ),
        in_specs=[smem, smem, anywhere, anywhere, anywhere, anywhere, vmem, vmem],
        out_specs=(vmem,) * 2,
        scratch_shapes=[
            pltpu.VMEM((HEADS * GROUP * ROWS, HEAD_SIZE), bf16),
            pltpu.VMEM((HEADS, nc, ny, nz, ROWS, HEAD_SIZE), bf16),
            pltpu.VMEM((ROWS, depth), bf16),
            pltpu.VMEM((ny, nz, nc, nx, sub, ROWS), bf16),
            pltpu.VMEM((depth, HIDDEN), bf16),
            pltpu.VMEM((nc * ny, nz * ROWS, GROUP * ROWS), bf16),
            pltpu.VMEM((nc * ny, 8, GROUP * ROWS), f32),
            pltpu.VMEM((nz, sub, plane * ROWS), bf16),
            pltpu.VMEM((nc, ny, nx, ROWS, HIDDEN), bf16),
            pltpu.VMEM((ROWS, HIDDEN), f32),
            pltpu.VMEM((ROWS, HIDDEN), f32),
            pltpu.VMEM((ROWS, HIDDEN), bf16),
            pltpu.VMEM((ns, HEADS, ROWS), f32),
            pltpu.VMEM((ns, HEADS, ROWS), f32),
            pltpu.VMEM((nz, 8, HIDDEN), f32),
            pltpu.VMEM((ny, 8, HIDDEN), f32),
            pltpu.VMEM((nc, 8, HIDDEN), f32),
            pltpu.VMEM((ndp, 8, HIDDEN), f32),
            pltpu.VMEM((nl, nz, sub, side_width), f32),
            pltpu.VMEM((column, sub, side_width), f32),
            pltpu.VMEM((nl, nx, sub, side_width), f32),
            pltpu.VMEM((ns, 1, 128), f32),
            pltpu.VMEM((ndp, 1, 128), f32),
            dma((HEADS * GROUP,)), dma((HEADS,)), dma((1,)), dma((CHUNKS,)),
            *key_sems, *slope_sems,
            dma((plane,)), dma((plane,)), dma((ns,)), dma((ns,)),
            dma((nz,)), dma((nz,)), dma((ny,)), dma((ny,)), dma((nc,)), dma((nc,)),
            dma((ndp,)), dma((ndp,)), dma((column,)), dma((column,)), dma((ndp,)), dma((ndp,)),
            dma((ns,)), dma((ns,)), dma((ndp,)), dma((ndp,)),
        ],
        compiler_params=pltpu.CompilerParams(
            collective_id=0, has_side_effects=True, vmem_limit_bytes=60 * 1024 * 1024
        ),
    )(
        order, b2, queries.reshape(ROWS, -1), key_rows.reshape(ROWS, -1),
        hidden.reshape(ROWS, depth), w1, b1.reshape(1, HIDDEN), w2,
    )
    mass, loss, step, second, first_bias, bias = pl.pallas_call(
        finish,
        out_shape=(
            jax.ShapeDtypeStruct((1, HEADS, ROWS), f32),
            jax.ShapeDtypeStruct((1, 1), f32),
            jax.ShapeDtypeStruct((wide, HIDDEN), f32),
            jax.ShapeDtypeStruct((HEADS, HIDDEN), f32),
            jax.ShapeDtypeStruct((1, HIDDEN), f32),
            jax.ShapeDtypeStruct((1, HEADS), f32),
        ),
        in_specs=[vmem, vmem],
        out_specs=(vmem,) * 6,
    )(step, small)
    return (
        mass, loss.reshape(()), step, second, first_bias.reshape(HIDDEN), bias.reshape(HEADS)
    )


def solution(mesh, dp_parts=DP_PARTS, seq_parts=SEQ_PARTS):
    in_specs = (P("dp", "seq", None),) * 3 + (P(),) * 5
    out_specs = (P("dp", None, "seq"), P(), P("seq", None), P(), P(), P())
    body = functools.partial(per_device, dp_parts, seq_parts)
    return jax.shard_map(
        body, mesh=mesh, in_specs=in_specs, out_specs=out_specs, check_vma=False
    )
```

time: 936 us -> 128 us (0.14)
  waiting for transfers between devices: 316 us -> 0 us
  blocking collectives: 212 us -> 0 us
  loops' own time: 174 us -> 0 us
  Pallas kernels: 0 us -> 127 us
  other arithmetic: 120 us -> 0 us
  local copies, waits for them, and re-layouts: 57.2 us -> 0 us
  matrix products: 31.2 us -> 0 us
  between operations: 16.7 us -> 0.64 us
    unnamed x5 -> x0, waiting for transfers between devices: 232 us -> none
    another operation x130 -> x0, loops' own time: 174 us -> none  [the longest x2 171 us: blockwise(): return lax.fori_loop(0, rows_here // inner, visit_block, carried)]
    psum x2 -> x0, blocking collectives: 148 us -> none  [the longest x1 77 us: per_device(): lax.psum((second_part, first_bias_part, bias_part, loss_part), ('dp', 'se...]
    pallas_call x0 -> x2, Pallas kernels: none -> 127 us  [the longest x1 125 us: per_device(): pl.pallas_call(functools.partial(kernel, dp_parts, seq_parts), out_shape=...]
    all_gather x2 -> x0, waiting for transfers between devices: 83.7 us -> none  [the longest x1 64.1 us: per_device(): keys_whole = lax.all_gather(local_key_rows, 'seq', axis=0, tiled=True)]
    reduce_min x128 -> x0, other arithmetic: 83.5 us -> none  [the longest x64 41.8 us: mass_step(): jnp.min(key_pos) > jnp.max(query_pos)]
    all_to_all x1 -> x0, blocking collectives: 63.8 us -> none  [per_device(): lax.all_to_all(tokens_in, 'seq', split_axis=1, concat_axis=0, tiled=True)]
    dot_general x41 -> x0, matrix products: 31.2 us -> none  [the longest x36 19.5 us: raw_scores(): jnp.einsum('tkgd,nkd->kgtn', head_queries, head_keys, preferred_element_t...]
  transfers between devices with their start and end apart: 4 -> 0, of which waited for: 3 -> 0; matrix products, arithmetic and copies ran while one was open for 2% -> 0% of each run, Pallas kernels for 0% -> 0%
where the time goes in v2:
time: 128 us
  Pallas kernels  127 us (99%)
    pallas_call x1, Pallas kernels, per_device(): pl.pallas_call(functools.partial(kernel, dp_parts, seq_parts), out_shape=...  125 us

profile of v2, /device:TPU:1, one launch (start us, length us, event | category | flops | bytes accessed | tf_op | source)
XLA Modules:
  0.0 127.6 jit_solution(12518354646776710201)
XLA Ops:
  0.6 125.1 %shard_map.127 = (f32[256,512]{1,0:T(8,128)}, f32[16,512]{1,0:T(8,128)}) custom-call(s32[64]{0:T(128)} %order_ref.1, f32[4]{0:T(128)} %b2_ref.1, bf16[128,4096]{1,0:T(8,128)(2,1)} %bitcast.8, bf16[128,512]{1,0:T(8,128)(2,1)} %bitcast.9, bf16[128,8192]{1,0:T(8,128)(2,1)} %bitcast.7, bf16[8192,512]{1,0:T(8,128)(2,1)} %w1_hbm.1, f32[1,512]{1,0:T(1,128)} %bitcast.10, ...), custom_call_target="tpu_custom_call" | custom-call | tf_op jit(solution)/shard_map/pallas_call | solution.py:653
  125.7 1.9 %shard_map.128 = (f32[1,4,128]{2,1,0:T(4,128)}, f32[1,1]{1,0:T(1,128)}, f32[256,512]{1,0:T(8,128)}, f32[4,512]{1,0:T(4,128)}, f32[1,512]{1,0:T(1,128)}, /*index=5*/f32[1,4]{1,0:T(1,128)}) custom-call(f32[256,512]{1,0:T(8,128)} %get-tuple-element.14.step_in, f32[16,512]{1,0:T(8,128)} %get-tuple-element.15.small_in), custom_call_target="tpu_custom_call" | custom-call | tf_op jit(solution)/shard_map/pallas_call | solution.py:699

commit v3 on v2

--- a/solution.py
+++ b/solution.py
@@ -65,17 +65,30 @@
         self.w, self.axis, self.view, self.sems, self.y_first = w, axis, view, sems, y_first
         self.b, self.nb = (w.z, w.nz) if axis == "z" else (w.x, w.nx)
 
-    def copy(self, block, stage, chunk, hop, device):
-        place = (chunk, hop)
-        return remote(
-            block, block, self.sems[2 * stage].at[place], self.sems[2 * stage + 1].at[place], device
-        )
+    def copy(self, block, stage, chunk, device):
+        send, recv = self.sems
+        return remote(block, block, send.at[chunk, stage], recv.at[chunk, stage], device)
+
+    def whole(self, chunk, stage):
+        w = self.w
+        y_step = stage == (0 if chunk in self.y_first else 1)
+        if stage == 2:
+            block = self.view(chunk, 1 - w.c)
+        elif (w.ny if y_step else self.nb) == 1:
+            return None
+        elif y_step:
+            rest = (self.b,) if stage == 0 else ()
+            block = self.view(chunk, w.c, pl.ds(0, w.ny - 1), *rest)
+        else:
+            at_y = w.y if stage == 0 else slice(None)
+            block = self.view(chunk, w.c, at_y, pl.ds(0, self.nb - 1))
+        return self.copy(block, stage, chunk, w.device(c=1 - w.c))
 
     def sent(self, chunk, stage):
         w = self.w
         y_step = stage == (0 if chunk in self.y_first else 1)
         if stage == 2:
-            return [(self.view(chunk, w.c), 0, w.device(c=1 - w.c))]
+            return [(self.view(chunk, w.c), w.device(c=1 - w.c))]
         if stage == 0:
             block = self.view(chunk, w.c, w.y, self.b)
         elif y_step:
@@ -83,39 +96,20 @@
         else:
             block = self.view(chunk, w.c, slice(None), self.b)
         if y_step:
-            return [(block, hop, w.device(y=ring(w.y, hop, w.ny))) for hop in range(1, w.ny)]
+            return [(block, w.device(y=ring(w.y, hop, w.ny))) for hop in range(1, w.ny)]
         return [
-            (block, hop, w.device(**{self.axis: ring(self.b, hop, self.nb)}))
+            (block, w.device(**{self.axis: ring(self.b, hop, self.nb)}))
             for hop in range(1, self.nb)
         ]
 
-    def received(self, chunk, stage):
-        w = self.w
-        y_step = stage == (0 if chunk in self.y_first else 1)
-        if stage == 2:
-            return [(self.view(chunk, 1 - w.c), 0)]
-        result = []
-        for hop in range(1, w.ny if y_step else self.nb):
-            if y_step:
-                at_y, at_b = ring(w.y, w.ny - hop, w.ny), self.b
-            else:
-                at_y, at_b = w.y, ring(self.b, self.nb - hop, self.nb)
-            if stage == 0:
-                block = self.view(chunk, w.c, at_y, at_b)
-            elif y_step:
-                block = self.view(chunk, w.c, at_y)
-            else:
-                block = self.view(chunk, w.c, slice(None), at_b)
-            result.append((block, hop))
-        return result
-
     def start(self, chunk, stage):
-        for block, hop, device in self.sent(chunk, stage):
-            self.copy(block, stage, chunk, hop, device).start()
+        for block, device in self.sent(chunk, stage):
+            self.copy(block, stage, chunk, device).start()
 
     def arrive(self, chunk, stage):
-        for block, hop in self.received(chunk, stage):
-            self.copy(block, stage, chunk, hop, self.w.device(c=1 - self.w.c)).wait_recv()
+        whole = self.whole(chunk, stage)
+        if whole is not None:
+            whole.wait_recv()
 
     def forward(self, chunk, stage):
         self.arrive(chunk, stage - 1)
@@ -123,8 +117,9 @@
 
     def drain(self, chunk):
         for stage in range(3):
-            for block, hop, device in self.sent(chunk, stage):
-                self.copy(block, stage, chunk, hop, device).wait_send()
+            whole = self.whole(chunk, stage)
+            if whole is not None:
+                whole.wait_send()
 
 
 def attend(head, order_ref, w, q_buf, k_buf, p_buf, m_buf, mass_out, before, middle):
@@ -136,10 +131,9 @@
     q_pos = jnp.where(lane < BLK, low, high) * BLK + lax.rem(lane, BLK)
     inner = lax.broadcasted_iota(jnp.int32, (BLK, ROWS), 0)
 
-    def visit(step, carried):
+    def visit(step, highest, summed):
         before(step)
-        highest, summed = carried
-        c, y = lax.rem(w.c + step // w.ny, w.nc), lax.rem(w.y + step, w.ny)
+        c, y = ring(w.c, step // w.ny, w.nc), ring(w.y, step % w.ny, w.ny)
         keys = k_buf[head, c, y].reshape(keys_here, HEAD_SIZE)
         pieces = []
         for part in range(keys_here // BLK):
@@ -163,26 +157,24 @@
         m_buf[step, 0:1, :] = highest
         return highest, jnp.concatenate(new_summed, axis=1)
 
-    start_state = (jnp.full((1, width), -1e30, jnp.float32), jnp.zeros((1, width), jnp.float32))
-    highest, summed = lax.fori_loop(0, steps, visit, start_state)
+    highest, summed = jnp.full((1, width), -1e30, jnp.float32), jnp.zeros((1, width), jnp.float32)
+    for step in range(steps):
+        highest, summed = visit(step, highest, summed)
     middle()
     inverse = 1.0 / (summed * GROUP)
     row = lax.broadcasted_iota(jnp.int32, (16, width), 0)
 
-    def collect(step, _):
+    for step in range(steps):
         scale = jnp.exp2((m_buf[step, 0:1, :] - highest) * SCALE2) * inverse
         coarse = scale.astype(jnp.bfloat16).astype(jnp.float32)
         both = jnp.where(row == 0, coarse, jnp.where(row == 1, scale - coarse, 0.0))
         mass = dot_t(both.astype(jnp.bfloat16), p_buf[step])
         line = mass[0:1, :] + mass[1:2, :]
-        c, y = lax.rem(w.c + step // w.ny, w.nc), lax.rem(w.y + step, w.ny)
+        c, y = ring(w.c, step // w.ny, w.nc), ring(w.y, step % w.ny, w.ny)
         for part in range(w.nz):
             mass_out[(y * w.nz + part) * w.nc + c, pl.ds(head, 1), :] = line[
                 :, part * ROWS : part * ROWS + ROWS
             ]
-        return _
-
-    lax.fori_loop(0, steps, collect, 0)
 
 
 def inverse_root(square_sum, entries):
@@ -201,7 +193,7 @@
     mass_out, mass_in, small_z, small_y, small_c, small_d,
     part_buf, piece_buf, full_buf, sq_seq, sq_dp,
     q_sem, k_sem, hs_sem, w1_sem,
-    kg0, kg1, kg2, kg3, kg4, kg5, sg0, sg1, sg2, sg3, sg4, sg5,
+    kg_send, kg_recv, sg_send, sg_recv,
     a_send, a_recv, m_send, m_recv, z_send, z_recv, y_send, y_recv, c_send, c_recv,
     d_send, d_recv, p_send, p_recv, f_send, f_recv, e_send, e_recv, g_send, g_recv,
 ):
@@ -221,13 +213,16 @@
         at = at + (slice(None),) * (4 - len(at))
         return s_buf.at[(*at, pl.ds(chunk * 128, 128))]
 
-    key_gather = Gather(w, "z", key_view, (), (kg0, kg1, kg2, kg3, kg4, kg5))
-    slope_gather = Gather(w, "x", slope_view, (1, 3), (sg0, sg1, sg2, sg3, sg4, sg5))
+    def all_of(ref, send, recv):
+        return remote(ref, ref, send.at[0], recv.at[0], w.device(c=1 - w.c))
+
+    key_gather = Gather(w, "z", key_view, (), (kg_send, kg_recv))
+    slope_gather = Gather(w, "x", slope_view, (1, 3), (sg_send, sg_recv))
 
     k_copies = [
         pltpu.make_async_copy(
             k_hbm.at[:, pl.ds(head * HEAD_SIZE, HEAD_SIZE)], key_view(head, w.c, w.y, w.z),
-            k_sem.at[head],
+            k_sem.at[0],
         )
         for head in range(HEADS)
     ]
@@ -291,7 +286,7 @@
         return pltpu.make_async_copy(
             q_hbm.at[:, pl.ds(pl.multiple_of(head * HEAD_SIZE, 128), HEAD_SIZE)],
             q_buf.at[pl.ds(pl.multiple_of(head * ROWS, ROWS), ROWS), :],
-            q_sem.at[head],
+            q_sem.at[0],
         )
 
     def q_start(head, _):
@@ -317,11 +312,10 @@
             turned[y, z, c, inside // per, pl.ds(start, 128), :] = value
         return _
 
-    for copy in k_copies:
-        copy.wait()
+    own_keys = k_buf.at[:, w.c, w.y, w.z]
+    pltpu.make_async_copy(own_keys, own_keys, k_sem.at[0]).wait()
     pl.semaphore_wait(barrier, ns - 1 + plane - 1 + ndp - 1 + column - 1)
-    for head in range(HEADS):
-        key_gather.start(head, 0)
+    key_gather.start(0, 0)
     hs_copy.wait()
 
     pre_buf[...] = jnp.broadcast_to(b1_ref[...], (ROWS, HIDDEN))
@@ -339,7 +333,8 @@
         lax.fori_loop(quarter * per_quarter, (quarter + 1) * per_quarter, turn, 0)
         if quarter:
             key_gather.forward(quarter - 1, 1)
-    key_gather.forward(CHUNKS - 1, 1)
+        if quarter + 1 < CHUNKS:
+            key_gather.start(quarter + 1, 0)
 
     pre = pre_buf[...]
     gate = 1.0 / (1.0 + jnp.exp(-pre))
@@ -351,7 +346,7 @@
     def a_copy(hop):
         x, y, c = in_plane(ring(own_plane, hop, plane))
         return remote(
-            turned.at[y, :, c, x], own_cols, a_send.at[hop], a_recv.at[hop],
+            turned.at[y, :, c, x], own_cols, a_send.at[0], a_recv.at[0],
             w.device(x=x, y=y, c=c),
         )
 
@@ -359,23 +354,22 @@
         a_copy(hop).start()
         return _
 
-    def q_wait(head, _):
-        q_copy(head).wait()
-        return _
-
-    lax.fori_loop(0, HEADS * GROUP, q_wait, 0)
+    pltpu.make_async_copy(q_buf, q_buf, q_sem.at[0]).wait()
     cols[:, :, pl.ds(pl.multiple_of(own_plane * ROWS, ROWS), ROWS)] = turned[w.y, :, w.c, w.x]
 
+    def first_steps(step):
+        if step == 1:
+            key_gather.forward(CHUNKS - 1, 1)
+            key_gather.forward(0, 2)
+        if step == w.ny:
+            key_gather.arrive(0, 2)
+
+    attend(
+        0, order_ref, w, q_buf, k_buf, p_buf, m_buf, mass_out, first_steps,
+        lambda: key_gather.forward(1, 2),
+    )
+
     def one_head(head, _):
-        def before(step):
-            @pl.when((head == 0) & (step == 1))
-            def _():
-                key_gather.forward(0, 2)
-
-            @pl.when(step == w.ny)
-            def _():
-                key_gather.arrive(head, 2)
-
         def middle():
             @pl.when(head < HEADS - 1)
             def _():
@@ -385,14 +379,17 @@
             def _():
                 lax.fori_loop(1, plane, a_start, 0)
 
-        attend(head, order_ref, w, q_buf, k_buf, p_buf, m_buf, mass_out, before, middle)
-        return _
-
-    lax.fori_loop(0, HEADS, one_head, 0)
+        key_gather.arrive(head, 2)
+        attend(
+            head, order_ref, w, q_buf, k_buf, p_buf, m_buf, mass_out, lambda step: None, middle
+        )
+        return _
+
+    lax.fori_loop(1, HEADS, one_head, 0)
 
     def m_copy(hop):
         to = ring(me, hop, ns)
-        return remote(mass_out.at[to], mass_in.at[hop], m_send.at[hop], m_recv.at[hop], (dp, to))
+        return remote(mass_out.at[to], mass_in.at[hop - 1], m_send.at[0], m_recv.at[0], (dp, to))
 
     def m_start(hop, _):
         m_copy(hop).start()
@@ -407,11 +404,10 @@
     for chunk in range(CHUNKS):
         key_gather.drain(chunk)
 
-    def m_add(hop, total):
-        m_copy(hop).wait_recv()
-        return total + mass_in[hop]
-
-    mass = lax.fori_loop(1, ns, m_add, mass_out[me])
+    all_of(mass_in.at[pl.ds(0, ns - 1)], m_send, m_recv).wait_recv()
+    mass = mass_out[me]
+    for at in range(ns - 1):
+        mass += mass_in[at]
     residue = predicted - jnp.log(1.0 + mass)
     out_grad = residue / length
     turned_grad = jnp.transpose(
@@ -428,7 +424,7 @@
 
     def exchange(buf, at, count, send, recv, device):
         return [
-            remote(buf.at[at], buf.at[at], send.at[hop], recv.at[hop], device(hop))
+            remote(buf.at[at], buf.at[at], send.at[0], recv.at[0], device(hop))
             for hop in range(1, count)
         ]
 
@@ -448,9 +444,9 @@
     def d_copies():
         return exchange(small_d, dp, ndp, d_send, d_recv, lambda hop: (ring(dp, hop, ndp), me))
 
-    def settle(copies, buf):
-        for copy in copies:
-            copy.wait_recv()
+    def settle(buf, send, recv):
+        if buf.shape[0] > 1:
+            all_of(buf.at[pl.ds(0, buf.shape[0] - 1)], send, recv).wait_recv()
         total = buf[0]
         for at in range(1, buf.shape[0]):
             total += buf[at]
@@ -471,30 +467,22 @@
     for copy in z_copies():
         copy.start()
 
-    def m_drain(hop, _):
-        m_copy(hop).wait_send()
-        return _
-
-    lax.fori_loop(1, ns, m_drain, 0)
+    all_of(mass_in.at[pl.ds(0, ns - 1)], m_send, m_recv).wait_send()
     for chunk in range(CHUNKS):
         slope_gather.forward(chunk, 1)
-    small_y[w.y] = settle(z_copies(), small_z)
+    small_y[w.y] = settle(small_z, z_send, z_recv)
     for copy in y_copies():
         copy.start()
     slope_gather.forward(0, 2)
     slope_gather.forward(1, 2)
 
-    def a_wait(hop, _):
-        a_copy(hop).wait()
-        return _
-
-    lax.fori_loop(1, plane, a_wait, 0)
+    all_of(cols.at[:, :, pl.ds(0, (plane - 1) * ROWS)], a_send, a_recv).wait()
 
     def p_copy(side, hop):
         to = ring(w.z, hop, w.nz)
         return remote(
             part_buf.at[side, to], piece_buf.at[own_column],
-            p_send.at[side * w.nz + hop], p_recv.at[w.l * w.nz + hop], w.device(z=to, l=side),
+            p_send.at[0], p_recv.at[0], w.device(z=to, l=side),
         )
 
     def each_piece(side, action):
@@ -507,13 +495,10 @@
     for side in range(w.nl):
         chunks = range(side * CHUNKS // w.nl, (side + 1) * CHUNKS // w.nl)
         for chunk in chunks:
+            if chunk >= 2:
+                slope_gather.forward(chunk, 2)
+        for chunk in chunks:
             slope_gather.arrive(chunk, 2)
-        if side == 0:
-            for chunk in range(2, CHUNKS):
-                slope_gather.forward(chunk, 2)
-            if w.nl == 1:
-                for chunk in range(2, CHUNKS):
-                    slope_gather.arrive(chunk, 2)
         columns = pl.ds(side * side_width, side_width)
         total = dot(
             cols[...].reshape(w.nz * sub, plane * ROWS),
@@ -522,28 +507,23 @@
         part_buf[side] = total.reshape(w.nz, sub, side_width)
         each_piece(side, lambda hop, side=side: p_copy(side, hop).start())
         if side == 0:
-            small_c[w.c] = settle(y_copies(), small_y)
+            small_c[w.c] = settle(small_y, y_send, y_recv)
             for copy in c_copies():
                 copy.start()
 
-    small_d[dp] = settle(c_copies(), small_c)
+    small_d[dp] = settle(small_c, c_send, c_recv)
     for copy in d_copies():
         copy.start()
     piece_buf[own_column] = part_buf[w.l, w.z]
     for chunk in range(CHUNKS):
         slope_gather.drain(chunk)
-    for copy in z_copies() + y_copies() + c_copies():
-        copy.wait_send()
-
-    def p_wait(other, hop):
-        at = ring(w.z, w.nz - hop, w.nz) * w.nl + other
-        remote(
-            piece_buf.at[at], piece_buf.at[at], p_send.at[other * w.nz + hop],
-            p_recv.at[other * w.nz + hop], w.device(c=1 - w.c),
-        ).wait_recv()
-
-    for other in range(w.nl):
-        each_piece(other, lambda hop, other=other: p_wait(other, hop))
+    for buf, send, recv in (
+        (small_z, z_send, z_recv), (small_y, y_send, y_recv), (small_c, c_send, c_recv)
+    ):
+        if buf.shape[0] > 1:
+            all_of(buf.at[pl.ds(0, buf.shape[0] - 1)], send, recv).wait_send()
+
+    all_of(piece_buf.at[pl.ds(0, column - 1)], p_send, p_recv).wait_recv()
     piece = piece_buf[0]
     for at in range(1, column):
         piece += piece_buf[at]
@@ -555,28 +535,24 @@
 
     def e_copy(hop):
         return remote(
-            sq_seq.at[me], sq_seq.at[me], e_send.at[hop], e_recv.at[hop], (dp, ring(me, hop, ns))
+            sq_seq.at[me], sq_seq.at[me], e_send.at[0], e_recv.at[0], (dp, ring(me, hop, ns))
         )
 
     def e_start(hop, _):
         e_copy(hop).start()
         return _
 
-    def e_wait(hop, _):
-        e_copy(hop).wait_recv()
-        return _
-
     lax.fori_loop(1, ns, e_start, 0)
-    full_buf[w.l, w.x] = piece
+    full_buf[dp] = piece
 
     def f_copy(hop):
-        own = full_buf.at[w.l, w.x]
-        return remote(own, own, f_send.at[hop], f_recv.at[hop], (ring(dp, hop, ndp), me))
+        own = full_buf.at[dp]
+        return remote(own, own, f_send.at[0], f_recv.at[0], (ring(dp, hop, ndp), me))
 
     for hop in range(1, ndp):
         f_copy(hop).start()
 
-    small = settle(d_copies(), small_d)
+    small = settle(small_d, d_send, d_recv)
     second = small[0:HEADS, :]
     small_ref[0:HEADS, :] = second * inverse_root(whole_sum(second * second), HEADS * HIDDEN)
     first_bias = small[4:5, :]
@@ -584,9 +560,8 @@
     small_ref[5:6, :] = small[5:6, :]
     small_ref[8 : 8 + HEADS, 0:ROWS] = mass
 
-    for side in range(w.nl):
-        each_piece(side, lambda hop, side=side: p_copy(side, hop).wait_send())
-    lax.fori_loop(1, ns, e_wait, 0)
+    all_of(piece_buf.at[pl.ds(0, column - 1)], p_send, p_recv).wait_send()
+    all_of(sq_seq.at[pl.ds(0, ns - 1)], e_send, e_recv).wait_recv()
     square = sq_seq[0]
     for at in range(1, ns):
         square += sq_seq[at]
@@ -594,34 +569,26 @@
 
     def g_copy(hop):
         return remote(
-            sq_dp.at[dp], sq_dp.at[dp], g_send.at[hop], g_recv.at[hop], (ring(dp, hop, ndp), me)
+            sq_dp.at[dp], sq_dp.at[dp], g_send.at[0], g_recv.at[0], (ring(dp, hop, ndp), me)
         )
 
     for hop in range(1, ndp):
         g_copy(hop).start()
-    for hop in range(1, ndp):
-        f_copy(hop).wait_recv()
-    for hop in range(1, ndp):
-        g_copy(hop).wait_recv()
+    all_of(full_buf.at[pl.ds(0, ndp - 1)], f_send, f_recv).wait_recv()
+    all_of(sq_dp.at[pl.ds(0, ndp - 1)], g_send, g_recv).wait_recv()
     square = sq_dp[0]
     for at in range(1, ndp):
         square += sq_dp[at]
     scale = inverse_root(whole_sum(square), depth * HIDDEN)
     for side in range(w.nl):
         step_ref[:, side * side_width : (side + 1) * side_width] = (
-            full_buf[side].reshape(wide, side_width) * scale
-        )
-
-    def e_drain(hop, _):
-        e_copy(hop).wait_send()
-        return _
-
-    lax.fori_loop(1, ns, e_drain, 0)
-    for copy in d_copies():
-        copy.wait_send()
-    for hop in range(1, ndp):
-        f_copy(hop).wait_send()
-        g_copy(hop).wait_send()
+            full_buf[side * w.nx : (side + 1) * w.nx].reshape(wide, side_width) * scale
+        )
+
+    all_of(sq_seq.at[pl.ds(0, ns - 1)], e_send, e_recv).wait_send()
+    all_of(small_d.at[pl.ds(0, ndp - 1)], d_send, d_recv).wait_send()
+    all_of(full_buf.at[pl.ds(0, ndp - 1)], f_send, f_recv).wait_send()
+    all_of(sq_dp.at[pl.ds(0, ndp - 1)], g_send, g_recv).wait_send()
 
 
 def finish(step_in, small_in, mass_ref, loss_ref, step_ref, second_ref, first_bias_ref, bias_ref):
@@ -648,8 +615,6 @@
         pl.BlockSpec(memory_space=pl.ANY),
     )
     dma = pltpu.SemaphoreType.DMA
-    key_sems = [dma((CHUNKS, n)) for n in (nz, nz, ny, ny, 1, 1)]
-    slope_sems = [dma((CHUNKS, max(nx, ny)))] * 4 + [dma((CHUNKS, 1))] * 2
     step, small = pl.pallas_call(
         functools.partial(kernel, dp_parts, seq_parts),
         out_shape=(
@@ -679,15 +644,11 @@
             pltpu.VMEM((ndp, 8, HIDDEN), f32),
             pltpu.VMEM((nl, nz, sub, side_width), f32),
             pltpu.VMEM((column, sub, side_width), f32),
-            pltpu.VMEM((nl, nx, sub, side_width), f32),
+            pltpu.VMEM((ndp, sub, side_width), f32),
             pltpu.VMEM((ns, 1, 128), f32),
             pltpu.VMEM((ndp, 1, 128), f32),
-            dma((HEADS * GROUP,)), dma((HEADS,)), dma((1,)), dma((CHUNKS,)),
-            *key_sems, *slope_sems,
-            dma((plane,)), dma((plane,)), dma((ns,)), dma((ns,)),
-            dma((nz,)), dma((nz,)), dma((ny,)), dma((ny,)), dma((nc,)), dma((nc,)),
-            dma((ndp,)), dma((ndp,)), dma((column,)), dma((column,)), dma((ndp,)), dma((ndp,)),
-            dma((ns,)), dma((ns,)), dma((ndp,)), dma((ndp,)),
+            dma((1,)), dma((1,)), dma((1,)), dma((CHUNKS,)),
+            *[dma((CHUNKS, 3))] * 4, *[dma((1,))] * 20,
         ],
         compiler_params=pltpu.CompilerParams(
             collective_id=0, has_side_effects=True, vmem_limit_bytes=60 * 1024 * 1024

time: 128 us -> 115 us (0.90)
  Pallas kernels: 127 us -> 114 us
    pallas_call x1, Pallas kernels: 125 us -> 112 us  [per_device(): pl.pallas_call(functools.partial(kernel, dp_parts, seq_parts), out_shape=...]
where the time goes in v3:
time: 115 us
  Pallas kernels  114 us (99%)
    pallas_call x1, Pallas kernels, per_device(): pl.pallas_call(functools.partial(kernel, dp_parts, seq_parts), out_shape=...  112 us

profile of v3, /device:TPU:1, one launch (start us, length us, event | category | flops | bytes accessed | tf_op | source)
XLA Modules:
  0.0 115.0 jit_solution(1290375362468335753)
XLA Ops:
  0.6 112.4 %shard_map.127 = (f32[256,512]{1,0:T(8,128)}, f32[16,512]{1,0:T(8,128)}) custom-call(s32[64]{0:T(128)} %order_ref.1, f32[4]{0:T(128)} %b2_ref.1, bf16[128,4096]{1,0:T(8,128)(2,1)} %bitcast.8, bf16[128,512]{1,0:T(8,128)(2,1)} %bitcast.9, bf16[128,8192]{1,0:T(8,128)(2,1)} %bitcast.7, bf16[8192,512]{1,0:T(8,128)(2,1)} %w1_hbm.1, f32[1,512]{1,0:T(1,128)} %bitcast.10, ...), custom_call_target="tpu_custom_call" | custom-call | tf_op jit(solution)/shard_map/pallas_call | solution.py:618
  113.1 1.9 %shard_map.128 = (f32[1,4,128]{2,1,0:T(4,128)}, f32[1,1]{1,0:T(1,128)}, f32[256,512]{1,0:T(8,128)}, f32[4,512]{1,0:T(4,128)}, f32[1,512]{1,0:T(1,128)}, /*index=5*/f32[1,4]{1,0:T(1,128)}) custom-call(f32[256,512]{1,0:T(8,128)} %get-tuple-element.14.step_in, f32[16,512]{1,0:T(8,128)} %get-tuple-element.15.small_in), custom_call_target="tpu_custom_call" | custom-call | tf_op jit(solution)/shard_map/pallas_call | solution.py:660

commit v4 on v3

--- a/solution.py
+++ b/solution.py
@@ -17,6 +17,7 @@
 HIDDEN = 512
 KEYS = 512
 CHUNKS = 4
+HIDE = -32768.0
 SCALE2 = HEAD_SIZE**-0.5 * math.log2(math.e)
 LAST = (((1,), (1,)), ((), ()))
 DP_PARTS = (2, 4)
@@ -71,10 +72,10 @@
 
     def whole(self, chunk, stage):
         w = self.w
+        if stage == 2:
+            return self.copy(self.view(chunk, 1 - w.c), stage, chunk, w.device(c=1 - w.c))
         y_step = stage == (0 if chunk in self.y_first else 1)
-        if stage == 2:
-            block = self.view(chunk, 1 - w.c)
-        elif (w.ny if y_step else self.nb) == 1:
+        if (w.ny if y_step else self.nb) == 1:
             return None
         elif y_step:
             rest = (self.b,) if stage == 0 else ()
@@ -122,7 +123,9 @@
                 whole.wait_send()
 
 
-def attend(head, order_ref, w, q_buf, k_buf, p_buf, m_buf, mass_out, before, middle):
+def attend(
+    head, order_ref, w, q_buf, k_buf, hide_buf, side_buf, p_buf, m_buf, mass_out, before, middle
+):
     steps = w.nc * w.ny
     keys_here = w.nz * ROWS
     width = GROUP * ROWS
@@ -135,17 +138,24 @@
         before(step)
         c, y = ring(w.c, step // w.ny, w.nc), ring(w.y, step % w.ny, w.ny)
         keys = k_buf[head, c, y].reshape(keys_here, HEAD_SIZE)
-        pieces = []
-        for part in range(keys_here // BLK):
-            owner = (y * w.nz + part // 2) * w.nc + c
-            k_pos = order_ref[2 * owner + part % 2] * BLK + inner
-            pieces.append(jnp.where(k_pos <= q_pos, 0.0, -1e30))
-        bias = jnp.concatenate(pieces, axis=0)
-        bias = jnp.concatenate([bias, bias], axis=1)
+        if step == 0:
+            pieces = []
+            for part in range(keys_here // BLK):
+                owner = (y * w.nz + part // 2) * w.nc + c
+                k_pos = order_ref[2 * owner + part % 2] * BLK + inner
+                pieces.append(jnp.where(k_pos <= q_pos, 0.0, -1e30))
+            bias = jnp.concatenate(pieces, axis=0)
+            bias = jnp.concatenate([bias, bias], axis=1)
+        else:
+            keys = jnp.concatenate([keys, hide_buf[step]], axis=1)
         new_highest, new_summed = [], []
         for pair in range(GROUP // 2):
             start = pl.multiple_of((head * GROUP + 2 * pair) * ROWS, 2 * ROWS)
-            score = dot_t(keys, q_buf[pl.ds(start, 2 * ROWS), :]) + bias
+            queries = q_buf[pl.ds(start, 2 * ROWS), :]
+            if step == 0:
+                score = dot_t(keys, queries) + bias
+            else:
+                score = dot_t(keys, jnp.concatenate([queries, side_buf[...]], axis=1))
             old = highest[:, pair * 256 : pair * 256 + 256]
             top = jnp.maximum(old, jnp.max(score, axis=0, keepdims=True))
             weight = jnp.exp2((score - top) * SCALE2)
@@ -189,7 +199,7 @@
     dp_parts, seq_parts,
     order_ref, b2_ref, q_hbm, k_hbm, hs_hbm, w1_hbm, b1_ref, w2_ref,
     step_ref, small_ref,
-    q_buf, k_buf, hs_buf, turned, w1_buf, p_buf, m_buf, cols, s_buf, pre_buf, gate_buf, hid_buf,
+    q_buf, k_buf, hide_buf, side_buf, hs_buf, turned, w1_buf, p_buf, m_buf, cols, s_buf, pre_buf, gate_buf, hid_buf,
     mass_out, mass_in, small_z, small_y, small_c, small_d,
     part_buf, piece_buf, full_buf, sq_seq, sq_dp,
     q_sem, k_sem, hs_sem, w1_sem,
@@ -216,7 +226,7 @@
     def all_of(ref, send, recv):
         return remote(ref, ref, send.at[0], recv.at[0], w.device(c=1 - w.c))
 
-    key_gather = Gather(w, "z", key_view, (), (kg_send, kg_recv))
+    key_gather = Gather(w, "z", key_view, (CHUNKS - 1,), (kg_send, kg_recv))
     slope_gather = Gather(w, "x", slope_view, (1, 3), (sg_send, sg_recv))
 
     k_copies = [
@@ -316,7 +326,25 @@
     pltpu.make_async_copy(own_keys, own_keys, k_sem.at[0]).wait()
     pl.semaphore_wait(barrier, ns - 1 + plane - 1 + ndp - 1 + column - 1)
     key_gather.start(0, 0)
+    key_gather.start(CHUNKS - 1, 0)
     hs_copy.wait()
+
+    low, high = order_ref[2 * me], order_ref[2 * me + 1]
+    line = lax.broadcasted_iota(jnp.int32, (BLK, 128), 1)
+    for step in range(1, w.nc * w.ny):
+        c, y = ring(w.c, step // w.ny, w.nc), ring(w.y, step % w.ny, w.ny)
+        for part in range(w.nz * ROWS // BLK):
+            block = order_ref[2 * ((y * w.nz + part // 2) * w.nc + c) + part % 2]
+            hide = jnp.where(
+                line == 0,
+                jnp.where(block > low, HIDE, 0.0),
+                jnp.where((line == 1) & (block > high), HIDE, 0.0),
+            )
+            hide_buf[step, part * BLK : part * BLK + BLK, :] = hide.astype(jnp.bfloat16)
+    row = lax.broadcasted_iota(jnp.int32, (2 * ROWS, 128), 0)
+    column_of = lax.rem(row, ROWS) // BLK
+    lane = lax.broadcasted_iota(jnp.int32, (2 * ROWS, 128), 1)
+    side_buf[...] = jnp.where(lane == column_of, 1.0, 0.0).astype(jnp.bfloat16)
 
     pre_buf[...] = jnp.broadcast_to(b1_ref[...], (ROWS, HIDDEN))
     per_quarter = depth // 128 // quarters
@@ -333,7 +361,7 @@
         lax.fori_loop(quarter * per_quarter, (quarter + 1) * per_quarter, turn, 0)
         if quarter:
             key_gather.forward(quarter - 1, 1)
-        if quarter + 1 < CHUNKS:
+        if quarter + 1 < CHUNKS - 1:
             key_gather.start(quarter + 1, 0)
 
     pre = pre_buf[...]
@@ -341,21 +369,33 @@
     gate_buf[...] = gate * (1.0 + pre * (1.0 - gate))
     hid_buf[...] = (pre * gate).astype(jnp.bfloat16)
 
-    own_cols = cols.at[:, :, pl.ds(pl.multiple_of(own_plane * ROWS, ROWS), ROWS)]
-
-    def a_copy(hop):
-        x, y, c = in_plane(ring(own_plane, hop, plane))
-        return remote(
-            turned.at[y, :, c, x], own_cols, a_send.at[0], a_recv.at[0],
-            w.device(x=x, y=y, c=c),
-        )
-
-    def a_start(hop, _):
-        a_copy(hop).start()
-        return _
+    own_cols = cols.at[own_plane]
+
+    def distance(step):
+        across, along, other = step
+        return (min(across, w.nx - across) + min(along, w.ny - along), across, along, other)
+
+    steps = [
+        (across, along, other)
+        for across in range(w.nx)
+        for along in range(w.ny)
+        for other in range(w.nc)
+        if across or along or other
+    ]
+    steps.sort(key=distance)
+
+    def a_start(over_y):
+        for across, along, other in steps:
+            if (along > 0) != over_y:
+                continue
+            x, y, c = ring(w.x, across, w.nx), ring(w.y, along, w.ny), ring(w.c, other, w.nc)
+            remote(
+                turned.at[y, :, c, x], own_cols, a_send.at[0], a_recv.at[0],
+                w.device(x=x, y=y, c=c),
+            ).start()
 
     pltpu.make_async_copy(q_buf, q_buf, q_sem.at[0]).wait()
-    cols[:, :, pl.ds(pl.multiple_of(own_plane * ROWS, ROWS), ROWS)] = turned[w.y, :, w.c, w.x]
+    cols[own_plane] = turned[w.y, :, w.c, w.x]
 
     def first_steps(step):
         if step == 1:
@@ -364,24 +404,29 @@
         if step == w.ny:
             key_gather.arrive(0, 2)
 
+    def first_middle():
+        key_gather.forward(1, 2)
+        a_start(False)
+
     attend(
-        0, order_ref, w, q_buf, k_buf, p_buf, m_buf, mass_out, first_steps,
-        lambda: key_gather.forward(1, 2),
+        0, order_ref, w, q_buf, k_buf, hide_buf, side_buf, p_buf, m_buf, mass_out, first_steps,
+        first_middle,
     )
 
     def one_head(head, _):
         def middle():
-            @pl.when(head < HEADS - 1)
-            def _():
-                key_gather.forward(head + 1, 2)
-
-            @pl.when(head == 1)
-            def _():
-                lax.fori_loop(1, plane, a_start, 0)
+            for other in range(1, HEADS - 1):
+
+                @pl.when(head == other)
+                def _():
+                    key_gather.forward(other + 1, 2)
+                    if other == 1:
+                        a_start(True)
 
         key_gather.arrive(head, 2)
         attend(
-            head, order_ref, w, q_buf, k_buf, p_buf, m_buf, mass_out, lambda step: None, middle
+            head, order_ref, w, q_buf, k_buf, hide_buf, side_buf, p_buf, m_buf, mass_out,
+            lambda step: None, middle,
         )
         return _
 
@@ -476,7 +521,7 @@
     slope_gather.forward(0, 2)
     slope_gather.forward(1, 2)
 
-    all_of(cols.at[:, :, pl.ds(0, (plane - 1) * ROWS)], a_send, a_recv).wait()
+    all_of(cols.at[pl.ds(0, plane - 1)], a_send, a_recv).wait()
 
     def p_copy(side, hop):
         to = ring(w.z, hop, w.nz)
@@ -501,7 +546,7 @@
             slope_gather.arrive(chunk, 2)
         columns = pl.ds(side * side_width, side_width)
         total = dot(
-            cols[...].reshape(w.nz * sub, plane * ROWS),
+            jnp.concatenate([cols[at].reshape(w.nz * sub, ROWS) for at in range(plane)], axis=1),
             s_buf[:, :, :, :, columns].reshape(plane * ROWS, side_width),
         )
         part_buf[side] = total.reshape(w.nz, sub, side_width)
@@ -626,12 +671,14 @@
         scratch_shapes=[
             pltpu.VMEM((HEADS * GROUP * ROWS, HEAD_SIZE), bf16),
             pltpu.VMEM((HEADS, nc, ny, nz, ROWS, HEAD_SIZE), bf16),
+            pltpu.VMEM((nc * ny, nz * ROWS, 128), bf16),
+            pltpu.VMEM((2 * ROWS, 128), bf16),
             pltpu.VMEM((ROWS, depth), bf16),
             pltpu.VMEM((ny, nz, nc, nx, sub, ROWS), bf16),
             pltpu.VMEM((depth, HIDDEN), bf16),
             pltpu.VMEM((nc * ny, nz * ROWS, GROUP * ROWS), bf16),
             pltpu.VMEM((nc * ny, 8, GROUP * ROWS), f32),
-            pltpu.VMEM((nz, sub, plane * ROWS), bf16),
+            pltpu.VMEM((plane, nz, sub, ROWS), bf16),
             pltpu.VMEM((nc, ny, nx, ROWS, HIDDEN), bf16),
             pltpu.VMEM((ROWS, HIDDEN), f32),
             pltpu.VMEM((ROWS, HIDDEN), f32),

time: 115 us -> 113 us (0.983)
    pallas_call x1, Pallas kernels: 112 us -> 111 us  [per_device(): pl.pallas_call(functools.partial(kernel, dp_parts, seq_parts), out_shape=...]
where the time goes in v4:
time: 113 us
  Pallas kernels  113 us (100%)
    pallas_call x1, Pallas kernels, per_device(): pl.pallas_call(functools.partial(kernel, dp_parts, seq_parts), out_shape=...  111 us

profile of v4, /device:TPU:1, one launch (start us, length us, event | category | flops | bytes accessed | tf_op | source)
XLA Modules:
  0.0 113.3 jit_solution(3910694261641081234)
XLA Ops:
  0.6 110.7 %shard_map.127 = (f32[256,512]{1,0:T(8,128)}, f32[16,512]{1,0:T(8,128)}) custom-call(s32[64]{0:T(128)} %order_ref.1, f32[4]{0:T(128)} %b2_ref.1, bf16[128,4096]{1,0:T(8,128)(2,1)} %bitcast.8, bf16[128,512]{1,0:T(8,128)(2,1)} %bitcast.9, bf16[128,8192]{1,0:T(8,128)(2,1)} %bitcast.7, bf16[8192,512]{1,0:T(8,128)(2,1)} %w1_hbm.1, f32[1,512]{1,0:T(1,128)} %bitcast.10, ...), custom_call_target="tpu_custom_call" | custom-call | tf_op jit(solution)/shard_map/pallas_call | solution.py:663
  111.4 1.9 %shard_map.128 = (f32[1,4,128]{2,1,0:T(4,128)}, f32[1,1]{1,0:T(1,128)}, f32[256,512]{1,0:T(8,128)}, f32[4,512]{1,0:T(4,128)}, f32[1,512]{1,0:T(1,128)}, /*index=5*/f32[1,4]{1,0:T(1,128)}) custom-call(f32[256,512]{1,0:T(8,128)} %get-tuple-element.14.step_in, f32[16,512]{1,0:T(8,128)} %get-tuple-element.15.small_in), custom_call_target="tpu_custom_call" | custom-call | tf_op jit(solution)/shard_map/pallas_call | solution.py:707
